TPU v7x, 32 devices: a whole 2x2x4 slice. The times are simulated.
32 devices in a mesh: grp: 2 (over x), lon: 16 (over z, y, core).
Axes of the slice: x: 2, y: 2, z: 4, core: 2. Of those that a mesh axis runs over, the one named last changes fastest.
Arguments:
- tracer_pert: float32 [4, 50, 32, 1024], P('grp', None, 'lon'), parts along dimension 0, may hold values from -60 to 60
- surface_pert: float32 [4, 32, 1024], P('grp', 'lon'), parts along dimension 0, may hold values from -60 to 60
- zonal_flow: float32 [50, 32, 1024], P(None, 'lon'), may hold values from -3.2 to 3.2
- merid_flow: float32 [50, 32, 1024], P(None, 'lon'), may hold values from -3.2 to 3.2
- bottom_level: int32 [32, 1024], P('lon'), may hold values from 0 to 50
Outputs:
- tracer_vec: float32 [4, 50, 32, 1024], P('grp', None, 'lon'), parts along dimension 0
- surface_vec: float32 [4, 32, 1024], P('grp', 'lon'), parts along dimension 0
- growth: float32 [6], P('grp'), parts along dimension 0
There are 2 independent parts, one for each index of `grp`. A program takes and returns all parts, laid end to end along the dimension named above; an argument that names none is the same for every part. Nothing has to cross between parts.
Inputs may be any that keep to these rules, and one draw needn't show every extreme that they name: `bottom_level`: 0 marks a land column, 50 a column wet to the bottom level.
All inputs are finite; a program needn't handle non-finite values.
Results may differ from a plain program's by a relative error of at most 0.0001.
Values sent between devices are 32-bit elements; how exact they have to be, the bound alone decides.
A program may use at most 64 MiB of HBM per device.

v0:
```python
import functools

import jax
import jax.numpy as jnp
from jax import lax
from jax.experimental import pallas as pl
from jax.experimental.pallas import tpu as pltpu
from jax.sharding import PartitionSpec as P

DIFFUSIVITY = 0.5
TIME_STEP = 0.2
SURFACE_COUPLING = 0.5
STERIC_GAIN = 2.0
EPSILON = 1e-06
MESH = pl.DeviceIdType.MESH
CHUNKS = 5
UNROLL = 5
SHIFTS = (1, -1, 2, -2)
SLOTS = 5
OWN = 2
CENTRES = (0.0, 0.04, 0.16, 0.64)
TILE = (8, 128)


def chunk_bounds(levels):
    count = min(CHUNKS, levels)
    edges = [levels * i // count for i in range(count + 1)]
    return list(zip(edges[:-1], edges[1:]))


def spread_rounds(n):
    reach, rounds = 2, []
    while 2 * reach < n:
        rounds.append(reach)
        reach *= 2
    return rounds


def shares_zonal(groups, levels):
    return groups == 2 and all((b - a) % 2 == 0 for a, b in chunk_bounds(levels))


def peers_loop(n, body):
    if n <= 16:
        for i in range(1, n):
            body(i)
    else:

        def step(i, carry):
            body(i)
            return carry

        lax.fori_loop(1, n, step, 0)


def kernel(
    n, share, trc_h, surf_h, zon_h, mer_h, bot_h, out, sout, gout,
    trc, surf, zon, mer, bot, s_t, r_t, s_z, r_z, s_b, r_b, coef, st, rx, red,
    in_sem, t_send, t_recv, z_send, z_recv, b_send, b_recv,
    st_send, st_recv, rx_send, rx_recv, rd_send, rd_recv, met,
):
    me = lax.axis_index("lon")
    grp = lax.axis_index("grp")
    levels = zon.shape[0]
    chunks = chunk_bounds(levels)
    side_dev = (lax.rem(me + n - 1, n), lax.rem(me + 1, n))
    outer = lax.rem(me, 2)
    inner = 1 - outer
    lane = lax.broadcasted_iota(jnp.int32, TILE, 1)
    row = lax.broadcasted_iota(jnp.int32, TILE, 0)
    last_lane, first_lane = lane == 127, lane == 0

    def north(x):
        rolled = pltpu.roll(x, 127, 1)
        return jnp.where(last_lane, pltpu.roll(rolled, 7, 0), rolled)

    def south(x):
        rolled = pltpu.roll(x, 1, 1)
        return jnp.where(first_lane, pltpu.roll(rolled, 1, 0), rolled)

    def col(c):
        return pl.ds(c, 8, stride=2)

    def lon_peer(s):
        return {"lon": lax.rem(me + s + n, n)}

    barrier = pltpu.get_barrier_semaphore()
    for s in SHIFTS:
        pl.semaphore_signal(barrier, inc=1, device_id=lon_peer(s), device_id_type=MESH)
    if share:
        pl.semaphore_signal(barrier, inc=1, device_id={"grp": 1 - grp}, device_id_type=MESH)

    def load(which, g):
        k0, k1 = chunks[g]
        ks = pl.ds(k0, k1 - k0)
        src, dst = (
            (zon_h.at[ks], zon.at[ks]),
            (trc_h.at[:, ks], trc.at[:, ks]),
            (mer_h.at[ks], mer.at[ks]),
        )[which]
        return pltpu.make_async_copy(src, dst, in_sem.at[which, g])

    count = len(chunks)
    load_bot = pltpu.make_async_copy(bot_h, bot, in_sem.at[3, 0])
    load_surf = pltpu.make_async_copy(surf_h, surf, in_sem.at[4, 0])
    load_bot.start()
    load_surf.start()
    for g in range(count):
        load(0, g).start()
        load(1, g).start()
    for g in range(count):
        load(2, g).start()
    load_bot.wait()
    load_surf.wait()
    for c in range(2):
        d = bot[col(c), :].astype(jnp.float32)
        st[OWN, 2 + c] = d
        for v in range(2):
            st[OWN, (4, 0)[c] + v] = jnp.where(d > 0, surf[v, col(c), :], 0.0)

    def gather_chunk(g):
        load(0, g).wait()
        load(1, g).wait()

        def step(k, carry):
            for c in range(2):
                s_t[c, k, 0] = trc[0, k, col(c), :]
                s_t[c, k, 1] = trc[1, k, col(c), :]
                s_z[c, k] = zon[k, col(c), :]
            return carry

        lax.fori_loop(*chunks[g], step, 0, unroll=UNROLL)

    def side_copy(src, dst, send, recv, g, side):
        k0, k1 = chunks[g]
        return pltpu.make_async_remote_copy(
            src_ref=src.at[side, pl.ds(k0, k1 - k0)],
            dst_ref=dst.at[1 - side, pl.ds(k0, k1 - k0)],
            send_sem=send.at[side, g],
            recv_sem=recv.at[1 - side, g],
            device_id={"lon": side_dev[side]},
            device_id_type=MESH,
        )

    def t_copy(g, side):
        return side_copy(s_t, r_t, t_send, t_recv, g, side)

    def b_copy(g, side):
        return side_copy(s_b, r_b, b_send, b_recv, g, side)

    def z_copies(g):
        if not share:
            return [side_copy(s_z, r_z, z_send, z_recv, g, side) for side in range(2)]
        k0, k1 = chunks[g]
        half = (k1 - k0) // 2
        mine = pl.ds(k0 + grp * half, half)
        across = pltpu.make_async_remote_copy(
            src_ref=s_z.at[outer, mine],
            dst_ref=r_z.at[1 - outer, mine],
            send_sem=z_send.at[0, g],
            recv_sem=z_recv.at[0, g],
            device_id=lon_peer(2 * outer - 1),
            device_id_type=MESH,
        )
        within = pltpu.make_async_remote_copy(
            src_ref=s_z.at[inner, pl.ds(k0, k1 - k0)],
            dst_ref=r_z.at[1 - inner, pl.ds(k0, k1 - k0)],
            send_sem=z_send.at[1, g],
            recv_sem=z_recv.at[1, g],
            device_id=lon_peer(2 * inner - 1),
            device_id_type=MESH,
        )
        onward = pltpu.make_async_remote_copy(
            src_ref=r_z.at[outer, mine],
            dst_ref=r_z.at[outer, mine],
            send_sem=z_send.at[2, g],
            recv_sem=z_recv.at[2, g],
            device_id={"grp": 1 - grp},
            device_id_type=MESH,
        )
        return [across, within, onward]

    def send_chunk(g):
        for copy in z_copies(g)[:2]:
            copy.start()
        for side in range(2):
            t_copy(g, side).start()

    def shift_copy(buf, send, recv, s, part):
        return pltpu.make_async_remote_copy(
            src_ref=buf.at[OWN, part],
            dst_ref=buf.at[OWN - s, part],
            send_sem=send.at[OWN - s],
            recv_sem=recv.at[OWN - s],
            device_id=lon_peer(s),
            device_id_type=MESH,
        )

    def st_copy(s):
        part = {1: pl.ds(0, 4), -1: pl.ds(2, 4), 2: pl.ds(3, 1), -2: pl.ds(2, 1)}[s]
        return shift_copy(st, st_send, st_recv, s, part)

    def rx_copy(s):
        part = {1: pl.ds(0, 4), -1: pl.ds(0, 4), 2: pl.ds(2, 2), -2: pl.ds(0, 2)}[s]
        return shift_copy(rx, rx_send, rx_recv, s, part)

    gather_chunk(0)
    pl.semaphore_wait(barrier, len(SHIFTS) + (1 if share else 0))
    for s in SHIFTS:
        st_copy(s).start()
    send_chunk(0)
    rounds = spread_rounds(n)

    def spread(i):
        if i < len(rounds):
            for s in (rounds[i], -rounds[i]):
                pl.semaphore_signal(
                    met.at[i], inc=1, device_id=lon_peer(s), device_id_type=MESH
                )

    def spread_wait(i):
        if i < len(rounds):
            pl.semaphore_wait(met.at[i], 2)

    spread(0)
    for g in range(1, count):
        gather_chunk(g)
        send_chunk(g)

    for s in SHIFTS:
        st_copy(s).wait_recv()

    depths = {-3: st[0, 3], -2: st[1, 2], -1: st[1, 3], 0: st[2, 2], 1: st[2, 3]}
    depths.update({2: st[3, 2], 3: st[3, 3], 4: st[4, 2]})

    def y_face(i):
        wall = jnp.logical_and(last_lane, row == 7)
        return jnp.where(wall, 0.0, jnp.minimum(depths[i], north(depths[i])))

    def x_face(i):
        return jnp.minimum(depths[i], depths[i + 1])

    half = TIME_STEP * 0.25
    diff = TIME_STEP * DIFFUSIVITY
    faces_x = [x_face(f - 1) for f in range(3)]
    faces_y = [y_face(c) for c in range(2)]
    own_depth = [depths[c] for c in range(2)]

    for g, (k0, k1) in enumerate(chunks):
        arrivals = z_copies(g)
        for copy in arrivals[:2]:
            copy.wait_recv()
        if share:
            arrivals[2].start()
        load(2, g).wait()
        for side in range(2):
            t_copy(g, side).wait_recv()
        if share:
            arrivals[2].wait_recv()

        def first(k, carry):
            kf = k.astype(jnp.float32)
            z = (r_z[0, k], s_z[0, k], s_z[1, k], r_z[1, k])
            cx = []
            for f in range(3):
                open_f = kf < faces_x[f]
                u = half * (z[f] + z[f + 1])
                cx.append((jnp.where(open_f, u + diff, 0.0), jnp.where(open_f, u - diff, 0.0)))
            cy = []
            for c in range(2):
                open_f = kf < faces_y[c]
                m = mer[k, col(c), :]
                u = half * (m + north(m))
                cy.append((jnp.where(open_f, u + diff, 0.0), jnp.where(open_f, u - diff, 0.0)))
            for q, (lo, hi) in enumerate(cx + cy):
                coef[k, 2 * q] = lo
                coef[k, 2 * q + 1] = hi
            wet = [kf < own_depth[c] for c in range(2)]
            for v in range(2):
                t = (
                    r_t[0, k, v],
                    jnp.where(wet[0], s_t[0, k, v], 0.0),
                    jnp.where(wet[1], s_t[1, k, v], 0.0),
                    r_t[1, k, v],
                )
                fx = [cx[f][0] * t[f] + cx[f][1] * t[f + 1] for f in range(3)]
                for c in range(2):
                    fy = cy[c][0] * t[c + 1] + cy[c][1] * north(t[c + 1])
                    s_b[c, k, v] = t[c + 1] - ((fx[c + 1] - fx[c]) + (fy - south(fy)))
            return carry

        lax.fori_loop(k0, k1, first, 0, unroll=UNROLL)
        for side in range(2):
            b_copy(g, side).start()
        spread_wait(g)
        spread(g + 1)
    for i in range(count, len(rounds)):
        spread_wait(i)
        spread(i + 1)

    face_x = {i: SURFACE_COUPLING * x_face(i) for i in range(-3, 4)}
    face_y = {i: SURFACE_COUPLING * y_face(i) for i in range(-2, 4)}

    def lap(s, cols):
        gx = {i: face_x[i] * (s[i + 1] - s[i]) for i in range(cols[0] - 1, cols[-1] + 1)}
        res = {}
        for i in cols:
            gy = face_y[i] * (north(s[i]) - s[i])
            res[i] = -((gx[i] - gx[i - 1]) + (gy - south(gy)))
        return res

    own = (0, 1)
    height = [{-1: st[1, v], 0: st[2, 4 + v], 1: st[2, v], 2: st[3, 4 + v]} for v in range(2)]
    lap_h = [lap(height[v], own) for v in range(2)]

    zero = jnp.zeros(TILE, jnp.float32)
    totals = (zero,) * 7
    for g, (k0, k1) in enumerate(chunks):
        for side in range(2):
            b_copy(g, side).wait_recv()

        def second(k, carry):
            sums, grams = list(carry[:4]), list(carry[4:])
            cx = [(coef[k, 2 * f], coef[k, 2 * f + 1]) for f in range(3)]
            cy = [(coef[k, 6 + 2 * c], coef[k, 7 + 2 * c]) for c in range(2)]
            new = []
            for v in range(2):
                t = (r_b[0, k, v], s_b[0, k, v], s_b[1, k, v], r_b[1, k, v])
                fx = [cx[f][0] * t[f] + cx[f][1] * t[f + 1] for f in range(3)]
                for c in range(2):
                    fy = cy[c][0] * t[c + 1] + cy[c][1] * north(t[c + 1])
                    val = t[c + 1] - ((fx[c + 1] - fx[c]) + (fy - south(fy)))
                    out[v, k, col(c), :] = val
                    sums[2 * v + c] = sums[2 * v + c] + val
                    new.append(val)
            grams[0] = grams[0] + (new[0] * new[0] + new[1] * new[1])
            grams[1] = grams[1] + (new[0] * new[2] + new[1] * new[3])
            grams[2] = grams[2] + (new[2] * new[2] + new[3] * new[3])
            return tuple(sums + grams)

        totals = lax.fori_loop(k0, k1, second, totals, unroll=UNROLL)

    gain = STERIC_GAIN / levels
    for v in range(2):
        for c in range(2):
            rx[OWN, 2 * c + v] = gain * totals[2 * v + c] - lap_h[v][c]
    for s in SHIFTS:
        rx_copy(s).start()

    def dot(a, b):
        return a[0] * b[0] + a[1] * b[1]

    parts = {}
    for q in range(3):
        parts["gram", q] = totals[4 + q]
    parts["hh", 0] = dot(height[0], height[0])
    parts["hh", 1] = dot(height[1], height[1])
    parts["hh", 2] = dot(height[0], height[1])
    for s in SHIFTS:
        rx_copy(s).wait_recv()

    span = 4.0 * levels
    powers = []
    for v in range(2):
        r = {-3: rx[0, 2 + v], 4: rx[4, v]}
        for c in range(2):
            r.update({c - 2: rx[1, 2 * c + v], c: rx[2, 2 * c + v], c + 2: rx[3, 2 * c + v]})
        l1 = lap(r, range(-2, 4))
        l2 = lap(l1, range(-1, 3))
        l3 = lap(l2, own)
        powers.append((r, l1, l2, l3))
    for v in range(2):
        for i, centre in enumerate(CENTRES):
            b = [{c: p[c] for c in own} for p in powers[v]]
            base = [b[0]]
            for j in range(3):
                if centre:
                    b = [
                        {c: b[q + 1][c] - (centre * span) * b[q][c] for c in own}
                        for q in range(3 - j)
                    ]
                else:
                    b = b[1:]
                base.append(b[0])
            for k in range(1 if i else 0, 6):
                parts["m", v, i, k] = dot(base[k // 2], base[(k + 1) // 2])
        for j in range(3):
            parts["h", v, v, j] = dot(height[v], powers[v][j])
            parts["h", v, 1 - v, j] = dot(height[v], powers[1 - v][j])
    for k in range(5):
        parts["c", k] = dot(powers[0][k // 2], powers[1][(k + 1) // 2])

    names = list(parts)
    level, shift = [parts[name] for name in names], 1
    while shift < 128:
        if len(level) == 1:
            level = [level[0] + pltpu.roll(level[0], shift, 1)]
        else:
            even = jnp.bitwise_and(lane, shift) == 0
            merged = []
            for i in range(0, len(level), 2):
                a, b = level[i], level[min(i + 1, len(level) - 1)]
                merged.append(jnp.where(even, a, b) + pltpu.roll(jnp.where(even, b, a), shift, 1))
            level = merged
        shift *= 2
    mine = level[0]
    for shift in (4, 2, 1):
        mine = mine + pltpu.roll(mine, shift, 0)
    red[me] = mine[0:1]

    def red_copy(i):
        return pltpu.make_async_remote_copy(
            src_ref=red.at[me],
            dst_ref=red.at[me],
            send_sem=rd_send,
            recv_sem=rd_recv,
            device_id=lon_peer(i),
            device_id_type=MESH,
        )

    def every(sem):
        return pltpu.make_async_copy(red.at[pl.ds(0, n - 1)], red.at[pl.ds(0, n - 1)], sem)

    peers_loop(n, lambda i: red_copy(i).start())
    every(rd_recv).wait()
    terms = [red[i] for i in range(n)]
    while len(terms) > 1:
        terms = [
            terms[i] + terms[i + 1] if i + 1 < len(terms) else terms[i]
            for i in range(0, len(terms), 2)
        ]
    total = {
        name: jnp.broadcast_to(terms[0][:, q : q + 1], TILE) for q, name in enumerate(names)
    }

    coefs = []
    for v in range(2):
        m0 = total["m", v, 0, 0]
        m = [m0] + [total["m", v, 0, k] for k in range(1, 6)]
        first_moment = m[1]
        centre = zero
        for i in range(1, len(CENTRES)):
            limit = 0.5 * (CENTRES[i] + CENTRES[i - 1]) * span
            above = first_moment > limit * m0
            centre = jnp.where(above, CENTRES[i] * span, centre)
            m = [m0] + [jnp.where(above, total["m", v, i, k], m[k]) for k in range(1, 6)]
        unit = 1.0 + centre
        a = [unit * m[k] + m[k + 1] for k in range(5)]
        ratio = m[1] / m0
        step0 = m0 / a[0]
        rr1 = step0 * step0 * (m[2] - ratio * m[1])
        beta0 = rr1 / m0
        along = step0 * ratio + beta0
        p1ap1 = along * along * a[0] - 2.0 * along * step0 * a[1] + step0 * step0 * a[2]
        step1 = rr1 / p1ap1
        x0 = step0 * ratio - step1 * along * unit
        x1 = step1 * step0 * unit - (step0 + step1 * along)
        x2 = step1 * step0

        def form(y0, y1, y2, f):
            return (
                y0 * (y0 * f[0] + 2.0 * (y1 * f[1] + y2 * f[2]))
                + y1 * (y1 * f[2] + 2.0 * (y2 * f[3]))
                + y2 * (y2 * f[4])
            )

        rr2 = form(x0, x1, x2, m)
        beta1 = rr2 / rr1
        y0, y1, y2 = x0 + beta1 * along, x1 - beta1 * step0, x2
        step2 = rr2 / form(y0, y1, y2, a)
        e0 = step0 + step1 * along + step2 * y0
        e1 = step2 * y1 - step1 * step0
        e2 = step2 * y2
        coefs.append((e0 - centre * (e1 - centre * e2), e1 - 2.0 * centre * e2, e2))
        for c in own:
            w = coefs[v]
            s = powers[v][0][c] * w[0] + (powers[v][1][c] * w[1] + powers[v][2][c] * w[2])
            sout[v, col(c), :] = height[v][c] + s

    def plain(v, k):
        return total["m", v, 0, k]

    gram = []
    for v in range(2):
        w = coefs[v]
        s = total["hh", v] + 2.0 * sum(w[j] * total["h", v, v, j] for j in range(3))
        for i in range(3):
            for j in range(3):
                s = s + w[i] * w[j] * plain(v, i + j)
        gram.append(total["gram", 2 * v] + s)
    mix = total["gram", 1] + total["hh", 2]
    for j in range(3):
        mix = mix + (coefs[1][j] * total["h", 0, 1, j] + coefs[0][j] * total["h", 1, 0, j])
    for i in range(3):
        for j in range(3):
            mix = mix + coefs[0][i] * coefs[1][j] * total["c", i + j]
    cells = float((levels + 1) * 2 * 8 * 128 * n)
    gram_one, gram_two, gram_mix = gram[0] / cells, gram[1] / cells, mix / cells
    scale_one = jnp.sqrt(gram_one + EPSILON)
    cross = gram_mix / scale_one
    rest = gram_two - 2.0 * cross * cross + cross * cross * gram_one / (gram_one + EPSILON)
    scale_two = jnp.sqrt(rest + EPSILON)
    gout[0] = 1.0 / scale_one
    gout[1] = cross
    gout[2] = 1.0 / scale_two
    gout[3] = jnp.where(lane == 0, scale_one, jnp.where(lane == 1, cross, scale_two))

    for g in range(count):
        for side in range(2):
            t_copy(g, side).wait_send()
            b_copy(g, side).wait_send()
        for copy in z_copies(g):
            copy.wait_send()
    for s in SHIFTS:
        st_copy(s).wait_send()
        rx_copy(s).wait_send()
    every(rd_send).wait()


def scale_kernel(trc, surf, tail, out_h, sout_h, gout, out, sout, sem):
    levels = trc.shape[1]
    chunks = chunk_bounds(levels)
    one, cross, two = tail[0], tail[1], tail[2]

    def store(g):
        k0, k1 = chunks[g]
        return pltpu.make_async_copy(
            out.at[:, pl.ds(k0, k1 - k0)], out_h.at[:, pl.ds(k0, k1 - k0)], sem.at[g]
        )

    for g, (k0, k1) in enumerate(chunks):

        def step(k, carry):
            for h in range(2):
                rows = pl.ds(8 * h, 8)
                unit = trc[0, k, rows, :] * one
                out[0, k, rows, :] = unit
                out[1, k, rows, :] = (trc[1, k, rows, :] - cross * unit) * two
            return carry

        lax.fori_loop(k0, k1, step, 0, unroll=UNROLL)
        store(g).start()
    for h in range(2):
        rows = pl.ds(8 * h, 8)
        unit = surf[0, rows, :] * one
        sout[0, rows, :] = unit
        sout[1, rows, :] = (surf[1, rows, :] - cross * unit) * two
    last = pltpu.make_async_copy(sout, sout_h, sem.at[len(chunks)])
    last.start()
    gout[...] = tail[3]
    for g in range(len(chunks)):
        store(g).wait()
    last.wait()


def packed(x):
    lead, (cols, rows) = x.shape[:-2], x.shape[-2:]
    x = x.reshape(lead + (cols, rows // 128, 128))
    x = jnp.swapaxes(x, -3, -2)
    return x.reshape(lead + (cols * (rows // 128), 128))


def unpacked(x, cols):
    lead, (rows, lanes) = x.shape[:-2], x.shape[-2:]
    x = x.reshape(lead + (rows // cols, cols, lanes))
    x = jnp.swapaxes(x, -3, -2)
    return x.reshape(lead + (cols, rows // cols * lanes))


def on_device(n, groups, tracer_pert, surface_pert, zonal_flow, merid_flow, bottom_level):
    vectors, levels, columns, rows = tracer_pert.shape
    count = len(chunk_bounds(levels))
    share = shares_zonal(groups, levels)
    f32 = jnp.float32
    vmem = pl.BlockSpec(memory_space=pltpu.VMEM)
    hbm = pl.BlockSpec(memory_space=pltpu.HBM)
    dma = pltpu.SemaphoreType.DMA
    zonal_sems = 3 if share else 2
    tracer, surface, tail = pl.pallas_call(
        functools.partial(kernel, n, share),
        out_shape=(
            jax.ShapeDtypeStruct((vectors, levels, 16, 128), f32),
            jax.ShapeDtypeStruct((vectors, 16, 128), f32),
            jax.ShapeDtypeStruct((4, 8, 128), f32),
        ),
        in_specs=[hbm] * 5,
        out_specs=(vmem,) * 3,
        scratch_shapes=[
            pltpu.VMEM((vectors, levels, 16, 128), f32),
            pltpu.VMEM((vectors, 16, 128), f32),
            pltpu.VMEM((levels, 16, 128), f32),
            pltpu.VMEM((levels, 16, 128), f32),
            pltpu.VMEM((16, 128), jnp.int32),
            pltpu.VMEM((2, levels, 2, 8, 128), f32),
            pltpu.VMEM((2, levels, 2, 8, 128), f32),
            pltpu.VMEM((2, levels, 8, 128), f32),
            pltpu.VMEM((2, levels, 8, 128), f32),
            pltpu.VMEM((2, levels, 2, 8, 128), f32),
            pltpu.VMEM((2, levels, 2, 8, 128), f32),
            pltpu.VMEM((levels, 10, 8, 128), f32),
            pltpu.VMEM((SLOTS, 6, 8, 128), f32),
            pltpu.VMEM((SLOTS, 4, 8, 128), f32),
            pltpu.VMEM((n, 1, 128), f32),
            dma((5, count)),
            dma((2, count)),
            dma((2, count)),
            dma((zonal_sems, count)),
            dma((zonal_sems, count)),
            dma((2, count)),
            dma((2, count)),
            dma((SLOTS,)),
            dma((SLOTS,)),
            dma((SLOTS,)),
            dma((SLOTS,)),
            dma(()),
            dma(()),
            pltpu.SemaphoreType.REGULAR((max(1, len(spread_rounds(n))),)),
        ],
        compiler_params=pltpu.CompilerParams(
            collective_id=0, has_side_effects=True, vmem_limit_bytes=40 * 1024 * 1024
        ),
    )(
        *(
            pltpu.with_memory_space_constraint(packed(x), pltpu.HBM)
            for x in (tracer_pert, surface_pert, zonal_flow, merid_flow, bottom_level)
        )
    )
    tracer, surface, growth = pl.pallas_call(
        scale_kernel,
        out_shape=(
            jax.ShapeDtypeStruct((vectors, levels, 16, 128), f32),
            jax.ShapeDtypeStruct((vectors, 16, 128), f32),
            jax.ShapeDtypeStruct((8, 128), f32),
        ),
        in_specs=[vmem] * 3,
        out_specs=(hbm, hbm, vmem),
        scratch_shapes=[
            pltpu.VMEM((vectors, levels, 16, 128), f32),
            pltpu.VMEM((vectors, 16, 128), f32),
            dma((count + 1,)),
        ],
        compiler_params=pltpu.CompilerParams(vmem_limit_bytes=16 * 1024 * 1024),
    )(tracer, surface, tail)
    return unpacked(tracer, columns), unpacked(surface, columns), growth[0, :3]


def solution(mesh):
    placed = (
        P("grp", None, "lon", None),
        P("grp", "lon", None),
        P(None, "lon", None),
        P(None, "lon", None),
        P("lon", None),
    )
    return jax.shard_map(
        functools.partial(on_device, mesh.shape["lon"], mesh.shape["grp"]),
        mesh=mesh,
        in_specs=placed,
        out_specs=(P("grp", None, "lon", None), P("grp", "lon", None), P("grp")),
        check_vma=False,
    )
```

profile of v0, /device:TPU:0, one launch (start us, length us, event | category | flops | bytes accessed | tf_op | source)
XLA Modules:
  0.0 44.7 jit_solution(13126537165856289187)
XLA Ops:
  0.6 42.6 %shard_map.76 = (f32[2,50,16,128]{3,2,1,0:T(8,128)S(1)}, f32[2,16,128]{2,1,0:T(8,128)S(1)}, f32[4,8,128]{2,1,0:T(8,128)S(1)}) custom-call(f32[2,50,16,128]{3,2,1,0:T(8,128)} %bitcast.37, f32[2,16,128]{2,1,0:T(8,128)} %bitcast.40, f32[50,16,128]{2,1,0:T(8,128)} %bitcast.38, f32[50,16,128]{2,1,0:T(8,128)} %bitcast.39, s32[16,128]{1,0:T(8,128)} %bitcast.41), custom_call_target="tpu_custom_call" | custom-call | tf_op jit(solution)/shard_map/pallas_call | solution.py:579
  43.2 1.0 %shard_map.77 = (f32[2,50,16,128]{3,2,1,0:T(8,128)}, f32[2,16,128]{2,1,0:T(8,128)}, f32[8,128]{1,0:T(8,128)S(1)}) custom-call(f32[2,50,16,128]{3,2,1,0:T(8,128)S(1)} %get-tuple-element.9.trc, f32[2,16,128]{2,1,0:T(8,128)S(1)} %get-tuple-element.10.surf, f32[4,8,128]{2,1,0:T(8,128)S(1)} %get-tuple-element.11.tail), custom_call_target="tpu_custom_call" | custom-call | tf_op jit(solution)/shard_map/pallas_call | solution.py:628
  44.2 0.5 %slice_bitcast_fusion = f32[3]{0:T(128)} fusion(f32[8,128]{1,0:T(8,128)S(1)} %get-tuple-element.14), kind=kLoop, calls=%fused_computation | loop fusion | bytes 24 | tf_op jit(solution)/shard_map/squeeze | solution.py:644
where the time goes:
time: 44.9 us; the launch traced here: 44.7 us
  Pallas kernels  43.5 us (97%)
  between operations  0.65 us (1%)
  local copies, waits for them, and re-layouts  0.51 us (1%)
    pallas_call x1, Pallas kernels, on_device(): pl.pallas_call(functools.partial(kernel, n, share), out_shape=(jax.ShapeD...  42.6 us
    pallas_call x1, Pallas kernels, on_device(): pl.pallas_call(scale_kernel, out_shape=(jax.ShapeDtypeStruct((vectors, le...  0.96 us

commit v1 on v0

--- a/solution.py
+++ b/solution.py
@@ -15,6 +15,7 @@
 MESH = pl.DeviceIdType.MESH
 CHUNKS = 5
 UNROLL = 5
+NEAR = (1, -1)
 SHIFTS = (1, -1, 2, -2)
 SLOTS = 5
 OWN = 2
@@ -29,7 +30,7 @@
 
 
 def spread_rounds(n):
-    reach, rounds = 2, []
+    reach, rounds = 1, []
     while 2 * reach < n:
         rounds.append(reach)
         reach *= 2
@@ -37,7 +38,7 @@
 
 
 def shares_zonal(groups, levels):
-    return groups == 2 and all((b - a) % 2 == 0 for a, b in chunk_bounds(levels))
+    return groups == 2 and levels % 2 == 0
 
 
 def peers_loop(n, body):
@@ -85,48 +86,44 @@
         return {"lon": lax.rem(me + s + n, n)}
 
     barrier = pltpu.get_barrier_semaphore()
-    for s in SHIFTS:
+    for s in NEAR:
         pl.semaphore_signal(barrier, inc=1, device_id=lon_peer(s), device_id_type=MESH)
     if share:
         pl.semaphore_signal(barrier, inc=1, device_id={"grp": 1 - grp}, device_id_type=MESH)
 
+    half = levels // 2
+    mine = pl.ds(grp * half if share else 0, half)
+    theirs = pl.ds((1 - grp) * half, half) if share else pl.ds(half, levels - half)
+
     def load(which, g):
         k0, k1 = chunks[g]
         ks = pl.ds(k0, k1 - k0)
-        src, dst = (
-            (zon_h.at[ks], zon.at[ks]),
-            (trc_h.at[:, ks], trc.at[:, ks]),
-            (mer_h.at[ks], mer.at[ks]),
-        )[which]
+        src, dst = ((trc_h.at[:, ks], trc.at[:, ks]), (mer_h.at[ks], mer.at[ks]))[which]
         return pltpu.make_async_copy(src, dst, in_sem.at[which, g])
 
     count = len(chunks)
+    load_zon = [
+        pltpu.make_async_copy(zon_h.at[ks], zon.at[ks], in_sem.at[2, i])
+        for i, ks in enumerate((mine, theirs))
+    ]
     load_bot = pltpu.make_async_copy(bot_h, bot, in_sem.at[3, 0])
-    load_surf = pltpu.make_async_copy(surf_h, surf, in_sem.at[4, 0])
+    load_surf = pltpu.make_async_copy(surf_h, surf, in_sem.at[3, 1])
+    load_zon[0].start()
     load_bot.start()
     load_surf.start()
+    load(0, 0).start()
+    load_zon[1].start()
+    for g in range(1, count):
+        load(0, g).start()
     for g in range(count):
-        load(0, g).start()
         load(1, g).start()
-    for g in range(count):
-        load(2, g).start()
-    load_bot.wait()
-    load_surf.wait()
-    for c in range(2):
-        d = bot[col(c), :].astype(jnp.float32)
-        st[OWN, 2 + c] = d
-        for v in range(2):
-            st[OWN, (4, 0)[c] + v] = jnp.where(d > 0, surf[v, col(c), :], 0.0)
-
     def gather_chunk(g):
         load(0, g).wait()
-        load(1, g).wait()
 
         def step(k, carry):
             for c in range(2):
                 s_t[c, k, 0] = trc[0, k, col(c), :]
                 s_t[c, k, 1] = trc[1, k, col(c), :]
-                s_z[c, k] = zon[k, col(c), :]
             return carry
 
         lax.fori_loop(*chunks[g], step, 0, unroll=UNROLL)
@@ -148,41 +145,42 @@
     def b_copy(g, side):
         return side_copy(s_b, r_b, b_send, b_recv, g, side)
 
-    def z_copies(g):
+    def gather_zonal(i):
+        load_zon[i].wait()
+        ks = (mine, theirs)[i]
+
+        def step(k, carry):
+            for c in range(2):
+                s_z[c, ks.start + k] = zon[ks.start + k, col(c), :]
+            return carry
+
+        lax.fori_loop(0, ks.size, step, 0, unroll=UNROLL)
+
+    def z_copy(which):
         if not share:
-            return [side_copy(s_z, r_z, z_send, z_recv, g, side) for side in range(2)]
-        k0, k1 = chunks[g]
-        half = (k1 - k0) // 2
-        mine = pl.ds(k0 + grp * half, half)
-        across = pltpu.make_async_remote_copy(
-            src_ref=s_z.at[outer, mine],
-            dst_ref=r_z.at[1 - outer, mine],
-            send_sem=z_send.at[0, g],
-            recv_sem=z_recv.at[0, g],
-            device_id=lon_peer(2 * outer - 1),
+            return pltpu.make_async_remote_copy(
+                src_ref=s_z.at[which],
+                dst_ref=r_z.at[1 - which],
+                send_sem=z_send.at[which],
+                recv_sem=z_recv.at[which],
+                device_id={"lon": side_dev[which]},
+                device_id_type=MESH,
+            )
+        src, dst, dev = (
+            (s_z.at[outer, mine], r_z.at[1 - outer, mine], lon_peer(2 * outer - 1)),
+            (s_z.at[inner], r_z.at[1 - inner], lon_peer(2 * inner - 1)),
+            (r_z.at[outer, mine], r_z.at[outer, mine], {"grp": 1 - grp}),
+        )[which]
+        return pltpu.make_async_remote_copy(
+            src_ref=src,
+            dst_ref=dst,
+            send_sem=z_send.at[which],
+            recv_sem=z_recv.at[which],
+            device_id=dev,
             device_id_type=MESH,
         )
-        within = pltpu.make_async_remote_copy(
-            src_ref=s_z.at[inner, pl.ds(k0, k1 - k0)],
-            dst_ref=r_z.at[1 - inner, pl.ds(k0, k1 - k0)],
-            send_sem=z_send.at[1, g],
-            recv_sem=z_recv.at[1, g],
-            device_id=lon_peer(2 * inner - 1),
-            device_id_type=MESH,
-        )
-        onward = pltpu.make_async_remote_copy(
-            src_ref=r_z.at[outer, mine],
-            dst_ref=r_z.at[outer, mine],
-            send_sem=z_send.at[2, g],
-            recv_sem=z_recv.at[2, g],
-            device_id={"grp": 1 - grp},
-            device_id_type=MESH,
-        )
-        return [across, within, onward]
 
     def send_chunk(g):
-        for copy in z_copies(g)[:2]:
-            copy.start()
         for side in range(2):
             t_copy(g, side).start()
 
@@ -204,11 +202,24 @@
         part = {1: pl.ds(0, 4), -1: pl.ds(0, 4), 2: pl.ds(2, 2), -2: pl.ds(0, 2)}[s]
         return shift_copy(rx, rx_send, rx_recv, s, part)
 
+    gather_zonal(0)
+    pl.semaphore_wait(barrier, len(NEAR) + (1 if share else 0))
+    if share:
+        z_copy(0).start()
+    load_bot.wait()
+    load_surf.wait()
+    for c in range(2):
+        d = bot[col(c), :].astype(jnp.float32)
+        st[OWN, 2 + c] = d
+        for v in range(2):
+            st[OWN, (4, 0)[c] + v] = jnp.where(d > 0, surf[v, col(c), :], 0.0)
+    for s in NEAR:
+        st_copy(s).start()
     gather_chunk(0)
-    pl.semaphore_wait(barrier, len(SHIFTS) + (1 if share else 0))
-    for s in SHIFTS:
-        st_copy(s).start()
     send_chunk(0)
+    gather_zonal(1)
+    for which in range(1 if share else 0, 2):
+        z_copy(which).start()
     rounds = spread_rounds(n)
 
     def spread(i):
@@ -227,11 +238,14 @@
         gather_chunk(g)
         send_chunk(g)
 
-    for s in SHIFTS:
+    spread_wait(0)
+    for s in SHIFTS[2:]:
+        st_copy(s).start()
+    spread(1)
+    for s in NEAR:
         st_copy(s).wait_recv()
 
-    depths = {-3: st[0, 3], -2: st[1, 2], -1: st[1, 3], 0: st[2, 2], 1: st[2, 3]}
-    depths.update({2: st[3, 2], 3: st[3, 3], 4: st[4, 2]})
+    depths = {-2: st[1, 2], -1: st[1, 3], 0: st[2, 2], 1: st[2, 3], 2: st[3, 2], 3: st[3, 3]}
 
     def y_face(i):
         wall = jnp.logical_and(last_lane, row == 7)
@@ -240,23 +254,21 @@
     def x_face(i):
         return jnp.minimum(depths[i], depths[i + 1])
 
-    half = TIME_STEP * 0.25
+    for which in range(2):
+        z_copy(which).wait_recv()
+    if share:
+        z_copy(2).start()
+        z_copy(2).wait_recv()
+    quarter = TIME_STEP * 0.25
     diff = TIME_STEP * DIFFUSIVITY
     faces_x = [x_face(f - 1) for f in range(3)]
     faces_y = [y_face(c) for c in range(2)]
     own_depth = [depths[c] for c in range(2)]
 
     for g, (k0, k1) in enumerate(chunks):
-        arrivals = z_copies(g)
-        for copy in arrivals[:2]:
-            copy.wait_recv()
-        if share:
-            arrivals[2].start()
-        load(2, g).wait()
+        load(1, g).wait()
         for side in range(2):
             t_copy(g, side).wait_recv()
-        if share:
-            arrivals[2].wait_recv()
 
         def first(k, carry):
             kf = k.astype(jnp.float32)
@@ -264,13 +276,13 @@
             cx = []
             for f in range(3):
                 open_f = kf < faces_x[f]
-                u = half * (z[f] + z[f + 1])
+                u = quarter * (z[f] + z[f + 1])
                 cx.append((jnp.where(open_f, u + diff, 0.0), jnp.where(open_f, u - diff, 0.0)))
             cy = []
             for c in range(2):
                 open_f = kf < faces_y[c]
                 m = mer[k, col(c), :]
-                u = half * (m + north(m))
+                u = quarter * (m + north(m))
                 cy.append((jnp.where(open_f, u + diff, 0.0), jnp.where(open_f, u - diff, 0.0)))
             for q, (lo, hi) in enumerate(cx + cy):
                 coef[k, 2 * q] = lo
@@ -292,11 +304,14 @@
         lax.fori_loop(k0, k1, first, 0, unroll=UNROLL)
         for side in range(2):
             b_copy(g, side).start()
-        spread_wait(g)
-        spread(g + 1)
-    for i in range(count, len(rounds)):
+        spread_wait(g + 1)
+        spread(g + 2)
+    for i in range(count + 1, len(rounds)):
         spread_wait(i)
         spread(i + 1)
+    for s in SHIFTS[2:]:
+        st_copy(s).wait_recv()
+    depths.update({-3: st[0, 3], 4: st[4, 2]})
 
     face_x = {i: SURFACE_COUPLING * x_face(i) for i in range(-3, 4)}
     face_y = {i: SURFACE_COUPLING * y_face(i) for i in range(-2, 4)}
@@ -403,10 +418,10 @@
                 merged.append(jnp.where(even, a, b) + pltpu.roll(jnp.where(even, b, a), shift, 1))
             level = merged
         shift *= 2
-    mine = level[0]
+    local = level[0]
     for shift in (4, 2, 1):
-        mine = mine + pltpu.roll(mine, shift, 0)
-    red[me] = mine[0:1]
+        local = local + pltpu.roll(local, shift, 0)
+    red[me] = local[0:1]
 
     def red_copy(i):
         return pltpu.make_async_remote_copy(
@@ -509,8 +524,8 @@
         for side in range(2):
             t_copy(g, side).wait_send()
             b_copy(g, side).wait_send()
-        for copy in z_copies(g):
-            copy.wait_send()
+    for which in range(3 if share else 2):
+        z_copy(which).wait_send()
     for s in SHIFTS:
         st_copy(s).wait_send()
         rx_copy(s).wait_send()
@@ -601,11 +616,11 @@
             pltpu.VMEM((SLOTS, 6, 8, 128), f32),
             pltpu.VMEM((SLOTS, 4, 8, 128), f32),
             pltpu.VMEM((n, 1, 128), f32),
-            dma((5, count)),
+            dma((4, max(2, count))),
             dma((2, count)),
             dma((2, count)),
-            dma((zonal_sems, count)),
-            dma((zonal_sems, count)),
+            dma((zonal_sems,)),
+            dma((zonal_sems,)),
             dma((2, count)),
             dma((2, count)),
             dma((SLOTS,)),

time: 44.9 us -> 38.2 us (0.85)
  Pallas kernels: 43.5 us -> 36.8 us
    pallas_call x1, Pallas kernels: 42.6 us -> 35.9 us  [on_device(): pl.pallas_call(functools.partial(kernel, n, share), out_shape=(jax.ShapeD...]
where the time goes in v1:
time: 38.2 us; the launch traced here: 38 us
  Pallas kernels  36.8 us (96%)
  between operations  0.65 us (2%)
  local copies, waits for them, and re-layouts  0.51 us (1%)
    pallas_call x1, Pallas kernels, on_device(): pl.pallas_call(functools.partial(kernel, n, share), out_shape=(jax.ShapeD...  35.9 us
    pallas_call x1, Pallas kernels, on_device(): pl.pallas_call(scale_kernel, out_shape=(jax.ShapeDtypeStruct((vectors, le...  0.96 us

profile of v1, /device:TPU:0, one launch (start us, length us, event | category | flops | bytes accessed | tf_op | source)
XLA Modules:
  0.0 38.0 jit_solution(6222327637672956304)
XLA Ops:
  0.6 35.9 %shard_map.76 = (f32[2,50,16,128]{3,2,1,0:T(8,128)S(1)}, f32[2,16,128]{2,1,0:T(8,128)S(1)}, f32[4,8,128]{2,1,0:T(8,128)S(1)}) custom-call(f32[2,50,16,128]{3,2,1,0:T(8,128)} %bitcast.37, f32[2,16,128]{2,1,0:T(8,128)} %bitcast.40, f32[50,16,128]{2,1,0:T(8,128)} %bitcast.38, f32[50,16,128]{2,1,0:T(8,128)} %bitcast.39, s32[16,128]{1,0:T(8,128)} %bitcast.41), custom_call_target="tpu_custom_call" | custom-call | tf_op jit(solution)/shard_map/pallas_call | solution.py:594
  36.5 1.0 %shard_map.77 = (f32[2,50,16,128]{3,2,1,0:T(8,128)}, f32[2,16,128]{2,1,0:T(8,128)}, f32[8,128]{1,0:T(8,128)S(1)}) custom-call(f32[2,50,16,128]{3,2,1,0:T(8,128)S(1)} %get-tuple-element.9.trc, f32[2,16,128]{2,1,0:T(8,128)S(1)} %get-tuple-element.10.surf, f32[4,8,128]{2,1,0:T(8,128)S(1)} %get-tuple-element.11.tail), custom_call_target="tpu_custom_call" | custom-call | tf_op jit(solution)/shard_map/pallas_call | solution.py:643
  37.5 0.5 %slice_bitcast_fusion = f32[3]{0:T(128)} fusion(f32[8,128]{1,0:T(8,128)S(1)} %get-tuple-element.14), kind=kLoop, calls=%fused_computation | loop fusion | bytes 24 | tf_op jit(solution)/shard_map/squeeze | solution.py:659

commit v2 on v1

--- a/solution.py
+++ b/solution.py
@@ -16,9 +16,8 @@
 CHUNKS = 5
 UNROLL = 5
 NEAR = (1, -1)
-SHIFTS = (1, -1, 2, -2)
-SLOTS = 5
-OWN = 2
+SLOT = {0: 0, 1: 1, 2: 2, 3: 3, -1: 4}
+WINDOW = (-2, -1, 0, 1)
 CENTRES = (0.0, 0.04, 0.16, 0.64)
 TILE = (8, 128)
 
@@ -186,21 +185,44 @@
 
     def shift_copy(buf, send, recv, s, part):
         return pltpu.make_async_remote_copy(
-            src_ref=buf.at[OWN, part],
-            dst_ref=buf.at[OWN - s, part],
-            send_sem=send.at[OWN - s],
-            recv_sem=recv.at[OWN - s],
+            src_ref=buf.at[0, part],
+            dst_ref=buf.at[SLOT[s], part],
+            send_sem=send.at[SLOT[s]],
+            recv_sem=recv.at[SLOT[s]],
             device_id=lon_peer(s),
             device_id_type=MESH,
         )
 
-    def st_copy(s):
-        part = {1: pl.ds(0, 4), -1: pl.ds(2, 4), 2: pl.ds(3, 1), -2: pl.ds(2, 1)}[s]
-        return shift_copy(st, st_send, st_recv, s, part)
-
-    def rx_copy(s):
-        part = {1: pl.ds(0, 4), -1: pl.ds(0, 4), 2: pl.ds(2, 2), -2: pl.ds(0, 2)}[s]
-        return shift_copy(rx, rx_send, rx_recv, s, part)
+    def shift_copies(buf, send, recv, cases, act):
+        for s, usual, closing in cases:
+            closes = me == (0 if act == "wait_recv" else n - s)
+            if usual == closing:
+                getattr(shift_copy(buf, send, recv, s, usual), act)()
+                continue
+            if usual is not None:
+
+                @pl.when(jnp.logical_not(closes))
+                def _():
+                    getattr(shift_copy(buf, send, recv, s, usual), act)()
+
+            @pl.when(closes)
+            def _():
+                getattr(shift_copy(buf, send, recv, s, closing), act)()
+
+    st_near = ((1, pl.ds(0, 4), pl.ds(0, 6)), (-1, pl.ds(2, 4), pl.ds(2, 4)))
+    st_far = ((2, pl.ds(3, 1), pl.ds(2, 2)), (3, None, pl.ds(3, 1)))
+    rx_all = (
+        (2, pl.ds(2, 2), pl.ds(0, 4)),
+        (3, None, pl.ds(2, 2)),
+        (1, pl.ds(0, 4), pl.ds(0, 4)),
+        (-1, pl.ds(0, 4), pl.ds(0, 4)),
+    )
+
+    def st_act(cases, act):
+        shift_copies(st, st_send, st_recv, cases, act)
+
+    def rx_act(act):
+        shift_copies(rx, rx_send, rx_recv, rx_all, act)
 
     gather_zonal(0)
     pl.semaphore_wait(barrier, len(NEAR) + (1 if share else 0))
@@ -210,11 +232,10 @@
     load_surf.wait()
     for c in range(2):
         d = bot[col(c), :].astype(jnp.float32)
-        st[OWN, 2 + c] = d
+        st[0, 2 + c] = d
         for v in range(2):
-            st[OWN, (4, 0)[c] + v] = jnp.where(d > 0, surf[v, col(c), :], 0.0)
-    for s in NEAR:
-        st_copy(s).start()
+            st[0, (4, 0)[c] + v] = jnp.where(d > 0, surf[v, col(c), :], 0.0)
+    st_act(st_near, "start")
     gather_chunk(0)
     send_chunk(0)
     gather_zonal(1)
@@ -239,13 +260,10 @@
         send_chunk(g)
 
     spread_wait(0)
-    for s in SHIFTS[2:]:
-        st_copy(s).start()
     spread(1)
-    for s in NEAR:
-        st_copy(s).wait_recv()
-
-    depths = {-2: st[1, 2], -1: st[1, 3], 0: st[2, 2], 1: st[2, 3], 2: st[3, 2], 3: st[3, 3]}
+    st_act(st_near, "wait_recv")
+
+    depths = {-2: st[1, 2], -1: st[1, 3], 0: st[0, 2], 1: st[0, 3], 2: st[4, 2], 3: st[4, 3]}
 
     def y_face(i):
         wall = jnp.logical_and(last_lane, row == 7)
@@ -304,29 +322,28 @@
         lax.fori_loop(k0, k1, first, 0, unroll=UNROLL)
         for side in range(2):
             b_copy(g, side).start()
-        spread_wait(g + 1)
-        spread(g + 2)
-    for i in range(count + 1, len(rounds)):
-        spread_wait(i)
-        spread(i + 1)
-    for s in SHIFTS[2:]:
-        st_copy(s).wait_recv()
-    depths.update({-3: st[0, 3], 4: st[4, 2]})
-
-    face_x = {i: SURFACE_COUPLING * x_face(i) for i in range(-3, 4)}
-    face_y = {i: SURFACE_COUPLING * y_face(i) for i in range(-2, 4)}
+    spread_wait(1)
+    st_act(st_far, "start")
+    spread(2)
+
+    face_x = {i: SURFACE_COUPLING * x_face(i) for i in range(-2, 3)}
+    face_y = {i: SURFACE_COUPLING * y_face(i) for i in range(-2, 3)}
 
     def lap(s, cols):
         gx = {i: face_x[i] * (s[i + 1] - s[i]) for i in range(cols[0] - 1, cols[-1] + 1)}
-        res = {}
+        res, rise = {}, {}
         for i in cols:
-            gy = face_y[i] * (north(s[i]) - s[i])
+            rise[i] = north(s[i]) - s[i]
+            gy = face_y[i] * rise[i]
             res[i] = -((gx[i] - gx[i - 1]) + (gy - south(gy)))
-        return res
+        return res, rise
 
     own = (0, 1)
-    height = [{-1: st[1, v], 0: st[2, 4 + v], 1: st[2, v], 2: st[3, 4 + v]} for v in range(2)]
-    lap_h = [lap(height[v], own) for v in range(2)]
+    height = [
+        {-2: st[1, 4 + v], -1: st[1, v], 0: st[0, 4 + v], 1: st[0, v], 2: st[4, 4 + v]}
+        for v in range(2)
+    ]
+    lap_h = [lap(height[v], own)[0] for v in range(2)]
 
     zero = jnp.zeros(TILE, jnp.float32)
     totals = (zero,) * 7
@@ -354,16 +371,31 @@
             return tuple(sums + grams)
 
         totals = lax.fori_loop(k0, k1, second, totals, unroll=UNROLL)
+        if g == (count - 1) // 2:
+            for i in range(2, len(rounds)):
+                spread_wait(i)
+                spread(i + 1)
 
     gain = STERIC_GAIN / levels
     for v in range(2):
         for c in range(2):
-            rx[OWN, 2 * c + v] = gain * totals[2 * v + c] - lap_h[v][c]
-    for s in SHIFTS:
-        rx_copy(s).start()
+            rx[0, 2 * c + v] = gain * totals[2 * v + c] - lap_h[v][c]
+    rx_act("start")
+    st_act(st_far, "wait_recv")
+    depths.update({-5: st[3, 3], -4: st[2, 2], -3: st[2, 3]})
+    for i in (-5, -4, -3):
+        face_x[i] = SURFACE_COUPLING * x_face(i)
+    for i in (-4, -3):
+        face_y[i] = SURFACE_COUPLING * y_face(i)
+
+    is_first, is_last = me == 0, me == n - 1
+
+    def gathered(term):
+        left = term(-2) + term(-1)
+        return jnp.where(is_first, left, 0.0) + jnp.where(is_last, 0.0, term(0) + term(1))
 
     def dot(a, b):
-        return a[0] * b[0] + a[1] * b[1]
+        return gathered(lambda i: a[i] * b[i])
 
     parts = {}
     for q in range(3):
@@ -371,34 +403,42 @@
     parts["hh", 0] = dot(height[0], height[0])
     parts["hh", 1] = dot(height[1], height[1])
     parts["hh", 2] = dot(height[0], height[1])
-    for s in SHIFTS:
-        rx_copy(s).wait_recv()
+    rx_act("wait_recv")
 
     span = 4.0 * levels
     powers = []
     for v in range(2):
-        r = {-3: rx[0, 2 + v], 4: rx[4, v]}
+        r = {-5: rx[3, 2 + v]}
         for c in range(2):
-            r.update({c - 2: rx[1, 2 * c + v], c: rx[2, 2 * c + v], c + 2: rx[3, 2 * c + v]})
-        l1 = lap(r, range(-2, 4))
-        l2 = lap(l1, range(-1, 3))
-        l3 = lap(l2, own)
-        powers.append((r, l1, l2, l3))
+            r.update({c - 4: rx[2, 2 * c + v], c - 2: rx[1, 2 * c + v]})
+            r.update({c: rx[0, 2 * c + v], c + 2: rx[4, 2 * c + v]})
+        l1, rise0 = lap(r, range(-4, 3))
+        l2, rise1 = lap(l1, range(-3, 2))
+        powers.append((r, l1, l2))
+        rise2 = {i: north(l2[i]) - l2[i] for i in WINDOW}
+        for i, centre in enumerate(CENTRES):
+            shift = centre * span
+            if i:
+                b1 = {c: l1[c] - shift * r[c] for c in WINDOW}
+                b2 = {c: (l2[c] - 2.0 * shift * l1[c]) + shift * shift * r[c] for c in range(-3, 2)}
+                up = {
+                    c: (rise2[c] - 2.0 * shift * rise1[c]) + shift * shift * rise0[c]
+                    for c in WINDOW
+                }
+            else:
+                b1, b2, up = l1, l2, rise2
+                parts["m", v, i, 0] = dot(r, r)
+            parts["m", v, i, 1] = dot(r, b1)
+            parts["m", v, i, 2] = dot(b1, b1)
+            parts["m", v, i, 3] = dot(b1, b2)
+            parts["m", v, i, 4] = dot(b2, b2)
+
+            def energy(c):
+                across = b2[c] - b2[c - 1]
+                return face_x[c - 1] * across * across + face_y[c] * up[c] * up[c]
+
+            parts["m", v, i, 5] = gathered(energy)
     for v in range(2):
-        for i, centre in enumerate(CENTRES):
-            b = [{c: p[c] for c in own} for p in powers[v]]
-            base = [b[0]]
-            for j in range(3):
-                if centre:
-                    b = [
-                        {c: b[q + 1][c] - (centre * span) * b[q][c] for c in own}
-                        for q in range(3 - j)
-                    ]
-                else:
-                    b = b[1:]
-                base.append(b[0])
-            for k in range(1 if i else 0, 6):
-                parts["m", v, i, k] = dot(base[k // 2], base[(k + 1) // 2])
         for j in range(3):
             parts["h", v, v, j] = dot(height[v], powers[v][j])
             parts["h", v, 1 - v, j] = dot(height[v], powers[1 - v][j])
@@ -460,7 +500,7 @@
             centre = jnp.where(above, CENTRES[i] * span, centre)
             m = [m0] + [jnp.where(above, total["m", v, i, k], m[k]) for k in range(1, 6)]
         unit = 1.0 + centre
-        a = [unit * m[k] + m[k + 1] for k in range(5)]
+        a = [unit * m[k] + m[k + 1] for k in range(4)] + [m[4] + m[5]]
         ratio = m[1] / m0
         step0 = m0 / a[0]
         rr1 = step0 * step0 * (m[2] - ratio * m[1])
@@ -526,16 +566,18 @@
             b_copy(g, side).wait_send()
     for which in range(3 if share else 2):
         z_copy(which).wait_send()
-    for s in SHIFTS:
-        st_copy(s).wait_send()
-        rx_copy(s).wait_send()
+    st_act(st_near + st_far, "wait_send")
+    rx_act("wait_send")
     every(rd_send).wait()
 
 
-def scale_kernel(trc, surf, tail, out_h, sout_h, gout, out, sout, sem):
+def scale_kernel(trc, surf, tail, out_h, sout_h, gout_h, out, sout, gvec, sem):
     levels = trc.shape[1]
     chunks = chunk_bounds(levels)
     one, cross, two = tail[0], tail[1], tail[2]
+    gvec[...] = tail[3, 0, :3]
+    grow = pltpu.make_async_copy(gvec, gout_h, sem.at[len(chunks) + 1])
+    grow.start()
 
     def store(g):
         k0, k1 = chunks[g]
@@ -562,10 +604,10 @@
         sout[1, rows, :] = (surf[1, rows, :] - cross * unit) * two
     last = pltpu.make_async_copy(sout, sout_h, sem.at[len(chunks)])
     last.start()
-    gout[...] = tail[3]
     for g in range(len(chunks)):
         store(g).wait()
     last.wait()
+    grow.wait()
 
 
 def packed(x):
@@ -613,8 +655,8 @@
             pltpu.VMEM((2, levels, 2, 8, 128), f32),
             pltpu.VMEM((2, levels, 2, 8, 128), f32),
             pltpu.VMEM((levels, 10, 8, 128), f32),
-            pltpu.VMEM((SLOTS, 6, 8, 128), f32),
-            pltpu.VMEM((SLOTS, 4, 8, 128), f32),
+            pltpu.VMEM((len(SLOT), 6, 8, 128), f32),
+            pltpu.VMEM((len(SLOT), 4, 8, 128), f32),
             pltpu.VMEM((n, 1, 128), f32),
             dma((4, max(2, count))),
             dma((2, count)),
@@ -623,10 +665,10 @@
             dma((zonal_sems,)),
             dma((2, count)),
             dma((2, count)),
-            dma((SLOTS,)),
-            dma((SLOTS,)),
-            dma((SLOTS,)),
-            dma((SLOTS,)),
+            dma((len(SLOT),)),
+            dma((len(SLOT),)),
+            dma((len(SLOT),)),
+            dma((len(SLOT),)),
             dma(()),
             dma(()),
             pltpu.SemaphoreType.REGULAR((max(1, len(spread_rounds(n))),)),
@@ -645,18 +687,19 @@
         out_shape=(
             jax.ShapeDtypeStruct((vectors, levels, 16, 128), f32),
             jax.ShapeDtypeStruct((vectors, 16, 128), f32),
-            jax.ShapeDtypeStruct((8, 128), f32),
+            jax.ShapeDtypeStruct((3,), f32),
         ),
         in_specs=[vmem] * 3,
-        out_specs=(hbm, hbm, vmem),
+        out_specs=(hbm,) * 3,
         scratch_shapes=[
             pltpu.VMEM((vectors, levels, 16, 128), f32),
             pltpu.VMEM((vectors, 16, 128), f32),
-            dma((count + 1,)),
+            pltpu.VMEM((3,), f32),
+            dma((count + 2,)),
         ],
         compiler_params=pltpu.CompilerParams(vmem_limit_bytes=16 * 1024 * 1024),
     )(tracer, surface, tail)
-    return unpacked(tracer, columns), unpacked(surface, columns), growth[0, :3]
+    return unpacked(tracer, columns), unpacked(surface, columns), growth
 
 
 def solution(mesh):

time: 38.2 us -> 37.5 us (0.982)
  local copies, waits for them, and re-layouts: 0.51 us -> 0 us
    squeeze x1 -> x0, local copies, waits for them, and re-layouts: 0.51 us -> none  [on_device(): growth[0, :3]]
where the time goes in v2:
time: 37.5 us; the launch traced here: 37.3 us
  Pallas kernels  36.7 us (98%)
  between operations  0.64 us (2%)
    pallas_call x1, Pallas kernels, on_device(): pl.pallas_call(functools.partial(kernel, n, share), out_shape=(jax.ShapeD...  35.7 us
    pallas_call x1, Pallas kernels, on_device(): pl.pallas_call(scale_kernel, out_shape=(jax.ShapeDtypeStruct((vectors, le...  0.97 us

profile of v2, /device:TPU:0, one launch (start us, length us, event | category | flops | bytes accessed | tf_op | source)
XLA Modules:
  0.0 37.3 jit_solution(9707258142517345240)
XLA Ops:
  0.6 35.7 %shard_map.76 = (f32[2,50,16,128]{3,2,1,0:T(8,128)S(1)}, f32[2,16,128]{2,1,0:T(8,128)S(1)}, f32[4,8,128]{2,1,0:T(8,128)S(1)}) custom-call(f32[2,50,16,128]{3,2,1,0:T(8,128)} %bitcast.35, f32[2,16,128]{2,1,0:T(8,128)} %bitcast.38, f32[50,16,128]{2,1,0:T(8,128)} %bitcast.36, f32[50,16,128]{2,1,0:T(8,128)} %bitcast.37, s32[16,128]{1,0:T(8,128)} %bitcast.39), custom_call_target="tpu_custom_call" | custom-call | tf_op jit(solution)/shard_map/pallas_call | solution.py:636
  36.4 1.0 %shard_map.77 = (f32[2,50,16,128]{3,2,1,0:T(8,128)}, f32[2,16,128]{2,1,0:T(8,128)}, f32[3]{0:T(128)}) custom-call(f32[2,50,16,128]{3,2,1,0:T(8,128)S(1)} %get-tuple-element.9.trc, f32[2,16,128]{2,1,0:T(8,128)S(1)} %get-tuple-element.10.surf, f32[4,8,128]{2,1,0:T(8,128)S(1)} %get-tuple-element.11.tail), custom_call_target="tpu_custom_call" | custom-call | tf_op jit(solution)/shard_map/pallas_call | solution.py:685

commit v3 on v2

--- a/solution.py
+++ b/solution.py
@@ -55,7 +55,7 @@
 
 def kernel(
     n, share, trc_h, surf_h, zon_h, mer_h, bot_h, out, sout, gout,
-    trc, surf, zon, mer, bot, s_t, r_t, s_z, r_z, s_b, r_b, coef, st, rx, red,
+    trc, surf, zon, mer, bot, s_t, r_t, s_z, r_z, s_b, r_b, coef, st, rx, red, flat,
     in_sem, t_send, t_recv, z_send, z_recv, b_send, b_recv,
     st_send, st_recv, rx_send, rx_recv, rd_send, rd_recv, met,
 ):
@@ -328,14 +328,15 @@
 
     face_x = {i: SURFACE_COUPLING * x_face(i) for i in range(-2, 3)}
     face_y = {i: SURFACE_COUPLING * y_face(i) for i in range(-2, 3)}
+    face_s = {i: south(face_y[i]) for i in face_y}
 
     def lap(s, cols):
         gx = {i: face_x[i] * (s[i + 1] - s[i]) for i in range(cols[0] - 1, cols[-1] + 1)}
         res, rise = {}, {}
         for i in cols:
             rise[i] = north(s[i]) - s[i]
-            gy = face_y[i] * rise[i]
-            res[i] = -((gx[i] - gx[i - 1]) + (gy - south(gy)))
+            fall = s[i] - south(s[i])
+            res[i] = (gx[i - 1] - gx[i]) + (face_s[i] * fall - face_y[i] * rise[i])
         return res, rise
 
     own = (0, 1)
@@ -387,6 +388,7 @@
         face_x[i] = SURFACE_COUPLING * x_face(i)
     for i in (-4, -3):
         face_y[i] = SURFACE_COUPLING * y_face(i)
+        face_s[i] = south(face_y[i])
 
     is_first, is_last = me == 0, me == n - 1
 
@@ -446,19 +448,18 @@
         parts["c", k] = dot(powers[0][k // 2], powers[1][(k + 1) // 2])
 
     names = list(parts)
-    level, shift = [parts[name] for name in names], 1
-    while shift < 128:
-        if len(level) == 1:
-            level = [level[0] + pltpu.roll(level[0], shift, 1)]
-        else:
-            even = jnp.bitwise_and(lane, shift) == 0
+    place = lane - 16 * row
+    local = zero
+    for q in range(0, len(names), 8):
+        level = [parts[name] for name in names[q : q + 8]]
+        for shift in (1, 2, 4):
+            even = jnp.bitwise_and(row, shift) == 0
             merged = []
             for i in range(0, len(level), 2):
                 a, b = level[i], level[min(i + 1, len(level) - 1)]
-                merged.append(jnp.where(even, a, b) + pltpu.roll(jnp.where(even, b, a), shift, 1))
+                merged.append(jnp.where(even, a, b) + pltpu.roll(jnp.where(even, b, a), shift, 0))
             level = merged
-        shift *= 2
-    local = level[0]
+        local = jnp.where(place == q // 8, jnp.sum(level[0], axis=1, keepdims=True), local)
     for shift in (4, 2, 1):
         local = local + pltpu.roll(local, shift, 0)
     red[me] = local[0:1]
@@ -484,8 +485,13 @@
             terms[i] + terms[i + 1] if i + 1 < len(terms) else terms[i]
             for i in range(0, len(terms), 2)
         ]
+    every_row = jnp.broadcast_to(terms[0], TILE)
+    for q in range(-(-len(names) // 8)):
+        picked = jnp.where(place == q, every_row, 0.0)
+        flat[q] = jnp.broadcast_to(jnp.sum(picked, axis=1, keepdims=True), TILE)
     total = {
-        name: jnp.broadcast_to(terms[0][:, q : q + 1], TILE) for q, name in enumerate(names)
+        name: jnp.broadcast_to(flat[q // 8, q % 8 : q % 8 + 1], TILE)
+        for q, name in enumerate(names)
     }
 
     coefs = []
@@ -658,6 +664,7 @@
             pltpu.VMEM((len(SLOT), 6, 8, 128), f32),
             pltpu.VMEM((len(SLOT), 4, 8, 128), f32),
             pltpu.VMEM((n, 1, 128), f32),
+            pltpu.VMEM((16, 8, 128), f32),
             dma((4, max(2, count))),
             dma((2, count)),
             dma((2, count)),

time: 37.5 us -> 37 us (0.987)
  Pallas kernels: 36.7 us -> 36.2 us
    pallas_call x1, Pallas kernels: 35.7 us -> 35.2 us  [on_device(): pl.pallas_call(functools.partial(kernel, n, share), out_shape=(jax.ShapeD...]
where the time goes in v3:
time: 37 us; the launch traced here: 36.8 us
  Pallas kernels  36.2 us (98%)
  between operations  0.64 us (2%)
    pallas_call x1, Pallas kernels, on_device(): pl.pallas_call(functools.partial(kernel, n, share), out_shape=(jax.ShapeD...  35.2 us
    pallas_call x1, Pallas kernels, on_device(): pl.pallas_call(scale_kernel, out_shape=(jax.ShapeDtypeStruct((vectors, le...  0.97 us

profile of v3, /device:TPU:0, one launch (start us, length us, event | category | flops | bytes accessed | tf_op | source)
XLA Modules:
  0.0 36.8 jit_solution(10603269782614079827)
XLA Ops:
  0.6 35.2 %shard_map.76 = (f32[2,50,16,128]{3,2,1,0:T(8,128)S(1)}, f32[2,16,128]{2,1,0:T(8,128)S(1)}, f32[4,8,128]{2,1,0:T(8,128)S(1)}) custom-call(f32[2,50,16,128]{3,2,1,0:T(8,128)} %bitcast.35, f32[2,16,128]{2,1,0:T(8,128)} %bitcast.38, f32[50,16,128]{2,1,0:T(8,128)} %bitcast.36, f32[50,16,128]{2,1,0:T(8,128)} %bitcast.37, s32[16,128]{1,0:T(8,128)} %bitcast.39), custom_call_target="tpu_custom_call" | custom-call | tf_op jit(solution)/shard_map/pallas_call | solution.py:642
  35.8 1.0 %shard_map.77 = (f32[2,50,16,128]{3,2,1,0:T(8,128)}, f32[2,16,128]{2,1,0:T(8,128)}, f32[3]{0:T(128)}) custom-call(f32[2,50,16,128]{3,2,1,0:T(8,128)S(1)} %get-tuple-element.9.trc, f32[2,16,128]{2,1,0:T(8,128)S(1)} %get-tuple-element.10.surf, f32[4,8,128]{2,1,0:T(8,128)S(1)} %get-tuple-element.11.tail), custom_call_target="tpu_custom_call" | custom-call | tf_op jit(solution)/shard_map/pallas_call | solution.py:692

commit v4 on v3

--- a/solution.py
+++ b/solution.py
@@ -16,9 +16,15 @@
 CHUNKS = 5
 UNROLL = 5
 NEAR = (1, -1)
-SLOT = {0: 0, 1: 1, 2: 2, 3: 3, -1: 4}
-WINDOW = (-2, -1, 0, 1)
 CENTRES = (0.0, 0.04, 0.16, 0.64)
+FAR = 4
+SLOT = {0: 0, **{s: s for s in range(1, FAR + 3)}, -1: FAR + 3}
+OWN = (0, 1)
+MOMENTS = (
+    [("m", v, i, k) for v in range(2) for i in range(len(CENTRES)) for k in range(1 if i else 0, 6)]
+    + [("h", v, w, j) for v in range(2) for w in range(2) for j in range(3)]
+    + [("c", k) for k in range(5)]
+)
 TILE = (8, 128)
 
 
@@ -55,7 +61,7 @@
 
 def kernel(
     n, share, trc_h, surf_h, zon_h, mer_h, bot_h, out, sout, gout,
-    trc, surf, zon, mer, bot, s_t, r_t, s_z, r_z, s_b, r_b, coef, st, rx, red, flat,
+    trc, surf, zon, mer, bot, s_t, r_t, s_z, r_z, s_b, r_b, coef, st, rx, red, flat, mo, pw,
     in_sem, t_send, t_recv, z_send, z_recv, b_send, b_recv,
     st_send, st_recv, rx_send, rx_recv, rd_send, rd_recv, met,
 ):
@@ -209,20 +215,29 @@
             def _():
                 getattr(shift_copy(buf, send, recv, s, closing), act)()
 
-    st_near = ((1, pl.ds(0, 4), pl.ds(0, 6)), (-1, pl.ds(2, 4), pl.ds(2, 4)))
-    st_far = ((2, pl.ds(3, 1), pl.ds(2, 2)), (3, None, pl.ds(3, 1)))
-    rx_all = (
-        (2, pl.ds(2, 2), pl.ds(0, 4)),
-        (3, None, pl.ds(2, 2)),
-        (1, pl.ds(0, 4), pl.ds(0, 4)),
-        (-1, pl.ds(0, 4), pl.ds(0, 4)),
+    every_tile = pl.ds(0, 6)
+    st_near = ((1, pl.ds(0, 4), every_tile), (-1, pl.ds(2, 4), pl.ds(2, 4)))
+    st_far = (
+        (2, pl.ds(3, 1), every_tile),
+        *((s, None, every_tile) for s in range(3, FAR + 1)),
+        (FAR + 1, None, pl.ds(2, 2)),
+        (FAR + 2, None, pl.ds(3, 1)),
+    )
+    rx_near = ((1, pl.ds(0, 4), pl.ds(0, 4)), (-1, pl.ds(0, 4), pl.ds(0, 4)))
+    rx_second = ((2, pl.ds(2, 2), pl.ds(0, 4)),)
+    rx_far = (
+        *((s, None, pl.ds(0, 4)) for s in range(3, FAR + 2)),
+        (FAR + 2, None, pl.ds(2, 2)),
     )
 
     def st_act(cases, act):
         shift_copies(st, st_send, st_recv, cases, act)
 
-    def rx_act(act):
-        shift_copies(rx, rx_send, rx_recv, rx_all, act)
+    def rx_act(cases, act):
+        shift_copies(rx, rx_send, rx_recv, cases, act)
+
+    near = me < n - FAR
+    to_near = lax.rem(me + 2, n) < n - FAR
 
     gather_zonal(0)
     pl.semaphore_wait(barrier, len(NEAR) + (1 if share else 0))
@@ -263,7 +278,8 @@
     spread(1)
     st_act(st_near, "wait_recv")
 
-    depths = {-2: st[1, 2], -1: st[1, 3], 0: st[0, 2], 1: st[0, 3], 2: st[4, 2], 3: st[4, 3]}
+    depths = {-2: st[1, 2], -1: st[1, 3], 0: st[0, 2], 1: st[0, 3]}
+    depths.update({2: st[SLOT[-1], 2], 3: st[SLOT[-1], 3]})
 
     def y_face(i):
         wall = jnp.logical_and(last_lane, row == 7)
@@ -323,12 +339,12 @@
         for side in range(2):
             b_copy(g, side).start()
     spread_wait(1)
-    st_act(st_far, "start")
     spread(2)
 
     face_x = {i: SURFACE_COUPLING * x_face(i) for i in range(-2, 3)}
     face_y = {i: SURFACE_COUPLING * y_face(i) for i in range(-2, 3)}
     face_s = {i: south(face_y[i]) for i in face_y}
+    shared_faces = list(face_x)
 
     def lap(s, cols):
         gx = {i: face_x[i] * (s[i + 1] - s[i]) for i in range(cols[0] - 1, cols[-1] + 1)}
@@ -339,12 +355,11 @@
             res[i] = (gx[i - 1] - gx[i]) + (face_s[i] * fall - face_y[i] * rise[i])
         return res, rise
 
-    own = (0, 1)
     height = [
-        {-2: st[1, 4 + v], -1: st[1, v], 0: st[0, 4 + v], 1: st[0, v], 2: st[4, 4 + v]}
+        {-1: st[1, v], 0: st[0, 4 + v], 1: st[0, v], 2: st[SLOT[-1], 4 + v]}
         for v in range(2)
     ]
-    lap_h = [lap(height[v], own)[0] for v in range(2)]
+    lap_h = [lap(height[v], OWN)[0] for v in range(2)]
 
     zero = jnp.zeros(TILE, jnp.float32)
     totals = (zero,) * 7
@@ -376,28 +391,140 @@
             for i in range(2, len(rounds)):
                 spread_wait(i)
                 spread(i + 1)
+            st_act(st_far, "start")
 
     gain = STERIC_GAIN / levels
     for v in range(2):
         for c in range(2):
             rx[0, 2 * c + v] = gain * totals[2 * v + c] - lap_h[v][c]
-    rx_act("start")
+    rx_act(rx_far, "start")
+
+    @pl.when(to_near)
+    def _():
+        rx_act(rx_second, "start")
+
+    rx_act(rx_near, "start")
     st_act(st_far, "wait_recv")
-    depths.update({-5: st[3, 3], -4: st[2, 2], -3: st[2, 3]})
-    for i in (-5, -4, -3):
-        face_x[i] = SURFACE_COUPLING * x_face(i)
-    for i in (-4, -3):
-        face_y[i] = SURFACE_COUPLING * y_face(i)
-        face_s[i] = south(face_y[i])
-
-    is_first, is_last = me == 0, me == n - 1
-
-    def gathered(term):
-        left = term(-2) + term(-1)
-        return jnp.where(is_first, left, 0.0) + jnp.where(is_last, 0.0, term(0) + term(1))
+
+    def add_faces(first, last):
+        for i in range(first, last):
+            face_x.setdefault(i, SURFACE_COUPLING * x_face(i))
+        for i in range(first + 1, last):
+            if i not in face_y:
+                face_y[i] = SURFACE_COUPLING * y_face(i)
+                face_s[i] = south(face_y[i])
+
+    span = 4.0 * levels
+
+    def operator_powers(v, cols):
+        l1, rise0 = lap(r_cols[v], range(cols[0] - 2, cols[-1] + 2))
+        l2, rise1 = lap(l1, range(cols[0] - 1, cols[-1] + 1))
+        return r_cols[v], l1, l2, rise0, rise1
+
+    def moments(cols, tall):
+        def gathered(term):
+            return functools.reduce(lambda a, b: a + b, [term(c) for c in cols])
+
+        def dot(a, b):
+            return gathered(lambda i: a[i] * b[i])
+
+        parts, powers = {}, []
+        for v in range(2):
+            r, l1, l2, rise0, rise1 = operator_powers(v, cols)
+            powers.append((r, l1, l2))
+            rise2 = {i: north(l2[i]) - l2[i] for i in cols}
+            for i, centre in enumerate(CENTRES):
+                shift = centre * span
+                if i:
+                    b1 = {c: l1[c] - shift * r[c] for c in cols}
+                    b2 = {
+                        c: (l2[c] - 2.0 * shift * l1[c]) + shift * shift * r[c]
+                        for c in range(cols[0] - 1, cols[-1] + 1)
+                    }
+                    up = {
+                        c: (rise2[c] - 2.0 * shift * rise1[c]) + shift * shift * rise0[c]
+                        for c in cols
+                    }
+                else:
+                    b1, b2, up = l1, l2, rise2
+                    parts["m", v, i, 0] = dot(r, r)
+                parts["m", v, i, 1] = dot(r, b1)
+                parts["m", v, i, 2] = dot(b1, b1)
+                parts["m", v, i, 3] = dot(b1, b2)
+                parts["m", v, i, 4] = dot(b2, b2)
+
+                def energy(c):
+                    across = b2[c] - b2[c - 1]
+                    return face_x[c - 1] * across * across + face_y[c] * up[c] * up[c]
+
+                parts["m", v, i, 5] = gathered(energy)
+        for v in range(2):
+            for w in range(2):
+                for j in range(3):
+                    parts["h", v, w, j] = dot(tall[v], powers[w][j])
+        for k in range(5):
+            parts["c", k] = dot(powers[0][k // 2], powers[1][(k + 1) // 2])
+        return parts, powers
+
+    def keep_powers(powers):
+        for v in range(2):
+            for j in range(3):
+                for c in OWN:
+                    pw[v, j, c] = powers[v][j][c]
+
+    def take_r(slot):
+        for v in range(2):
+            for c in range(2):
+                r_cols[v][(2 if slot == SLOT[-1] else -2 * slot) + c] = rx[slot, 2 * c + v]
+
+    r_cols = [{}, {}]
+
+    @pl.when(near)
+    def _():
+        rx_act(rx_near + rx_second, "wait_recv")
+        depths[-3] = st[2, 3]
+        add_faces(-3, 3)
+        for slot in (0, 1, SLOT[-1]):
+            take_r(slot)
+        for v in range(2):
+            r_cols[v][-3] = rx[2, 2 + v]
+        parts, powers = moments(OWN, height)
+        for q, name in enumerate(MOMENTS):
+            mo[q] = parts[name]
+        keep_powers(powers)
+
+    @pl.when(jnp.logical_not(near))
+    def _():
+        for q in range(len(MOMENTS)):
+            mo[q] = zero
+
+    for known in (face_x, face_y, face_s):
+        for i in [i for i in known if i not in shared_faces]:
+            del known[i]
+
+    @pl.when(me == 0)
+    def _():
+        rx_act(rx_far, "wait_recv")
+        tall = [{}, {}]
+        for slot in range(1, FAR + 3):
+            for c in range(2):
+                depths[c - 2 * slot] = st[slot, 2 + c]
+        for slot in range(FAR + 3):
+            take_r(slot)
+        for slot in range(1, FAR + 1):
+            for v in range(2):
+                tall[v].update({-2 * slot: st[slot, 4 + v], 1 - 2 * slot: st[slot, v]})
+        add_faces(-2 * FAR - 3, 1)
+        parts, _ = moments(range(-2 * FAR, 0), tall)
+        for q, name in enumerate(MOMENTS):
+            mo[q] = mo[q] + parts[name]
+
+    for known in (face_x, face_y, face_s):
+        for i in [i for i in known if i not in shared_faces]:
+            del known[i]
 
     def dot(a, b):
-        return gathered(lambda i: a[i] * b[i])
+        return a[0] * b[0] + a[1] * b[1]
 
     parts = {}
     for q in range(3):
@@ -405,47 +532,8 @@
     parts["hh", 0] = dot(height[0], height[0])
     parts["hh", 1] = dot(height[1], height[1])
     parts["hh", 2] = dot(height[0], height[1])
-    rx_act("wait_recv")
-
-    span = 4.0 * levels
-    powers = []
-    for v in range(2):
-        r = {-5: rx[3, 2 + v]}
-        for c in range(2):
-            r.update({c - 4: rx[2, 2 * c + v], c - 2: rx[1, 2 * c + v]})
-            r.update({c: rx[0, 2 * c + v], c + 2: rx[4, 2 * c + v]})
-        l1, rise0 = lap(r, range(-4, 3))
-        l2, rise1 = lap(l1, range(-3, 2))
-        powers.append((r, l1, l2))
-        rise2 = {i: north(l2[i]) - l2[i] for i in WINDOW}
-        for i, centre in enumerate(CENTRES):
-            shift = centre * span
-            if i:
-                b1 = {c: l1[c] - shift * r[c] for c in WINDOW}
-                b2 = {c: (l2[c] - 2.0 * shift * l1[c]) + shift * shift * r[c] for c in range(-3, 2)}
-                up = {
-                    c: (rise2[c] - 2.0 * shift * rise1[c]) + shift * shift * rise0[c]
-                    for c in WINDOW
-                }
-            else:
-                b1, b2, up = l1, l2, rise2
-                parts["m", v, i, 0] = dot(r, r)
-            parts["m", v, i, 1] = dot(r, b1)
-            parts["m", v, i, 2] = dot(b1, b1)
-            parts["m", v, i, 3] = dot(b1, b2)
-            parts["m", v, i, 4] = dot(b2, b2)
-
-            def energy(c):
-                across = b2[c] - b2[c - 1]
-                return face_x[c - 1] * across * across + face_y[c] * up[c] * up[c]
-
-            parts["m", v, i, 5] = gathered(energy)
-    for v in range(2):
-        for j in range(3):
-            parts["h", v, v, j] = dot(height[v], powers[v][j])
-            parts["h", v, 1 - v, j] = dot(height[v], powers[1 - v][j])
-    for k in range(5):
-        parts["c", k] = dot(powers[0][k // 2], powers[1][(k + 1) // 2])
+    for q, name in enumerate(MOMENTS):
+        parts[name] = mo[q]
 
     names = list(parts)
     place = lane - 16 * row
@@ -478,6 +566,18 @@
         return pltpu.make_async_copy(red.at[pl.ds(0, n - 1)], red.at[pl.ds(0, n - 1)], sem)
 
     peers_loop(n, lambda i: red_copy(i).start())
+
+    @pl.when(jnp.logical_not(near))
+    def _():
+        rx_act(rx_near, "wait_recv")
+        for slot in (0, 1, SLOT[-1]):
+            take_r(slot)
+        powers = []
+        for v in range(2):
+            l1 = lap(r_cols[v], range(-1, 3))[0]
+            powers.append((r_cols[v], l1, lap(l1, OWN)[0]))
+        keep_powers(powers)
+
     every(rd_recv).wait()
     terms = [red[i] for i in range(n)]
     while len(terms) > 1:
@@ -533,9 +633,9 @@
         e1 = step2 * y1 - step1 * step0
         e2 = step2 * y2
         coefs.append((e0 - centre * (e1 - centre * e2), e1 - 2.0 * centre * e2, e2))
-        for c in own:
+        for c in OWN:
             w = coefs[v]
-            s = powers[v][0][c] * w[0] + (powers[v][1][c] * w[1] + powers[v][2][c] * w[2])
+            s = pw[v, 0, c] * w[0] + (pw[v, 1, c] * w[1] + pw[v, 2, c] * w[2])
             sout[v, col(c), :] = height[v][c] + s
 
     def plain(v, k):
@@ -573,7 +673,12 @@
     for which in range(3 if share else 2):
         z_copy(which).wait_send()
     st_act(st_near + st_far, "wait_send")
-    rx_act("wait_send")
+    rx_act(rx_near + rx_far, "wait_send")
+
+    @pl.when(to_near)
+    def _():
+        rx_act(rx_second, "wait_send")
+
     every(rd_send).wait()
 
 
@@ -665,6 +770,8 @@
             pltpu.VMEM((len(SLOT), 4, 8, 128), f32),
             pltpu.VMEM((n, 1, 128), f32),
             pltpu.VMEM((16, 8, 128), f32),
+            pltpu.VMEM((len(MOMENTS), 8, 128), f32),
+            pltpu.VMEM((2, 3, 2, 8, 128), f32),
             dma((4, max(2, count))),
             dma((2, count)),
             dma((2, count)),

time: 37 us -> 36.4 us (0.984)
  Pallas kernels: 36.2 us -> 35.6 us
    pallas_call x1, Pallas kernels: 35.2 us -> 34.6 us  [on_device(): pl.pallas_call(functools.partial(kernel, n, share), out_shape=(jax.ShapeD...]
where the time goes in v4:
time: 36.4 us; the launch traced here: 36.2 us
  Pallas kernels  35.6 us (98%)
  between operations  0.64 us (2%)
    pallas_call x1, Pallas kernels, on_device(): pl.pallas_call(functools.partial(kernel, n, share), out_shape=(jax.ShapeD...  34.6 us
    pallas_call x1, Pallas kernels, on_device(): pl.pallas_call(scale_kernel, out_shape=(jax.ShapeDtypeStruct((vectors, le...  0.97 us

profile of v4, /device:TPU:0, one launch (start us, length us, event | category | flops | bytes accessed | tf_op | source)
XLA Modules:
  0.0 36.2 jit_solution(7769018490022051131)
XLA Ops:
  0.6 34.6 %shard_map.76 = (f32[2,50,16,128]{3,2,1,0:T(8,128)S(1)}, f32[2,16,128]{2,1,0:T(8,128)S(1)}, f32[4,8,128]{2,1,0:T(8,128)S(1)}) custom-call(f32[2,50,16,128]{3,2,1,0:T(8,128)} %bitcast.35, f32[2,16,128]{2,1,0:T(8,128)} %bitcast.38, f32[50,16,128]{2,1,0:T(8,128)} %bitcast.36, f32[50,16,128]{2,1,0:T(8,128)} %bitcast.37, s32[16,128]{1,0:T(8,128)} %bitcast.39), custom_call_target="tpu_custom_call" | custom-call | tf_op jit(solution)/shard_map/pallas_call | solution.py:747
  35.3 1.0 %shard_map.77 = (f32[2,50,16,128]{3,2,1,0:T(8,128)}, f32[2,16,128]{2,1,0:T(8,128)}, f32[3]{0:T(128)}) custom-call(f32[2,50,16,128]{3,2,1,0:T(8,128)S(1)} %get-tuple-element.9.trc, f32[2,16,128]{2,1,0:T(8,128)S(1)} %get-tuple-element.10.surf, f32[4,8,128]{2,1,0:T(8,128)S(1)} %get-tuple-element.11.tail), custom_call_target="tpu_custom_call" | custom-call | tf_op jit(solution)/shard_map/pallas_call | solution.py:799

commit v5 on v4

--- a/solution.py
+++ b/solution.py
@@ -14,7 +14,7 @@
 EPSILON = 1e-06
 MESH = pl.DeviceIdType.MESH
 CHUNKS = 5
-UNROLL = 5
+UNROLL = 10
 NEAR = (1, -1)
 CENTRES = (0.0, 0.04, 0.16, 0.64)
 FAR = 4
@@ -28,10 +28,8 @@
 TILE = (8, 128)
 
 
-def chunk_bounds(levels):
-    count = min(CHUNKS, levels)
-    edges = [levels * i // count for i in range(count + 1)]
-    return list(zip(edges[:-1], edges[1:]))
+def chunk_count(levels):
+    return max(c for c in range(1, CHUNKS + 1) if levels % c == 0)
 
 
 def spread_rounds(n):
@@ -68,7 +66,8 @@
     me = lax.axis_index("lon")
     grp = lax.axis_index("grp")
     levels = zon.shape[0]
-    chunks = chunk_bounds(levels)
+    count = chunk_count(levels)
+    size = levels // count
     side_dev = (lax.rem(me + n - 1, n), lax.rem(me + 1, n))
     outer = lax.rem(me, 2)
     inner = 1 - outer
@@ -100,13 +99,19 @@
     mine = pl.ds(grp * half if share else 0, half)
     theirs = pl.ds((1 - grp) * half, half) if share else pl.ds(half, levels - half)
 
+    def chunk(g):
+        return pl.ds(g * size, size)
+
+    def in_chunk(g, body, carry):
+        return lax.fori_loop(
+            0, size, lambda i, state: body(g * size + i, state), carry, unroll=min(UNROLL, size)
+        )
+
     def load(which, g):
-        k0, k1 = chunks[g]
-        ks = pl.ds(k0, k1 - k0)
+        ks = chunk(g)
         src, dst = ((trc_h.at[:, ks], trc.at[:, ks]), (mer_h.at[ks], mer.at[ks]))[which]
         return pltpu.make_async_copy(src, dst, in_sem.at[which, g])
 
-    count = len(chunks)
     load_zon = [
         pltpu.make_async_copy(zon_h.at[ks], zon.at[ks], in_sem.at[2, i])
         for i, ks in enumerate((mine, theirs))
@@ -131,13 +136,12 @@
                 s_t[c, k, 1] = trc[1, k, col(c), :]
             return carry
 
-        lax.fori_loop(*chunks[g], step, 0, unroll=UNROLL)
+        in_chunk(g, step, 0)
 
     def side_copy(src, dst, send, recv, g, side):
-        k0, k1 = chunks[g]
         return pltpu.make_async_remote_copy(
-            src_ref=src.at[side, pl.ds(k0, k1 - k0)],
-            dst_ref=dst.at[1 - side, pl.ds(k0, k1 - k0)],
+            src_ref=src.at[side, chunk(g)],
+            dst_ref=dst.at[1 - side, chunk(g)],
             send_sem=send.at[side, g],
             recv_sem=recv.at[1 - side, g],
             device_id={"lon": side_dev[side]},
@@ -159,7 +163,7 @@
                 s_z[c, ks.start + k] = zon[ks.start + k, col(c), :]
             return carry
 
-        lax.fori_loop(0, ks.size, step, 0, unroll=UNROLL)
+        lax.fori_loop(0, ks.size, step, 0, unroll=5)
 
     def z_copy(which):
         if not share:
@@ -270,9 +274,12 @@
             pl.semaphore_wait(met.at[i], 2)
 
     spread(0)
-    for g in range(1, count):
+
+    @pl.loop(1, count)
+    def _(g):
         gather_chunk(g)
         send_chunk(g)
+
 
     spread_wait(0)
     spread(1)
@@ -299,7 +306,8 @@
     faces_y = [y_face(c) for c in range(2)]
     own_depth = [depths[c] for c in range(2)]
 
-    for g, (k0, k1) in enumerate(chunks):
+    @pl.loop(0, count)
+    def _(g):
         load(1, g).wait()
         for side in range(2):
             t_copy(g, side).wait_recv()
@@ -335,7 +343,7 @@
                     s_b[c, k, v] = t[c + 1] - ((fx[c + 1] - fx[c]) + (fy - south(fy)))
             return carry
 
-        lax.fori_loop(k0, k1, first, 0, unroll=UNROLL)
+        in_chunk(g, first, 0)
         for side in range(2):
             b_copy(g, side).start()
     spread_wait(1)
@@ -362,8 +370,8 @@
     lap_h = [lap(height[v], OWN)[0] for v in range(2)]
 
     zero = jnp.zeros(TILE, jnp.float32)
-    totals = (zero,) * 7
-    for g, (k0, k1) in enumerate(chunks):
+
+    def second_chunk(g, totals):
         for side in range(2):
             b_copy(g, side).wait_recv()
 
@@ -386,12 +394,14 @@
             grams[2] = grams[2] + (new[2] * new[2] + new[3] * new[3])
             return tuple(sums + grams)
 
-        totals = lax.fori_loop(k0, k1, second, totals, unroll=UNROLL)
-        if g == (count - 1) // 2:
-            for i in range(2, len(rounds)):
-                spread_wait(i)
-                spread(i + 1)
-            st_act(st_far, "start")
+        return in_chunk(g, second, totals)
+
+    totals = lax.fori_loop(0, count // 2 + 1, second_chunk, (zero,) * 7)
+    for i in range(2, len(rounds)):
+        spread_wait(i)
+        spread(i + 1)
+    st_act(st_far, "start")
+    totals = lax.fori_loop(count // 2 + 1, count, second_chunk, totals)
 
     gain = STERIC_GAIN / levels
     for v in range(2):
@@ -666,10 +676,13 @@
     gout[2] = 1.0 / scale_two
     gout[3] = jnp.where(lane == 0, scale_one, jnp.where(lane == 1, cross, scale_two))
 
-    for g in range(count):
+
+    @pl.loop(0, count)
+    def _(g):
         for side in range(2):
             t_copy(g, side).wait_send()
             b_copy(g, side).wait_send()
+
     for which in range(3 if share else 2):
         z_copy(which).wait_send()
     st_act(st_near + st_far, "wait_send")
@@ -684,21 +697,21 @@
 
 def scale_kernel(trc, surf, tail, out_h, sout_h, gout_h, out, sout, gvec, sem):
     levels = trc.shape[1]
-    chunks = chunk_bounds(levels)
+    count = chunk_count(levels)
+    size = levels // count
     one, cross, two = tail[0], tail[1], tail[2]
     gvec[...] = tail[3, 0, :3]
-    grow = pltpu.make_async_copy(gvec, gout_h, sem.at[len(chunks) + 1])
+    grow = pltpu.make_async_copy(gvec, gout_h, sem.at[count + 1])
     grow.start()
 
     def store(g):
-        k0, k1 = chunks[g]
-        return pltpu.make_async_copy(
-            out.at[:, pl.ds(k0, k1 - k0)], out_h.at[:, pl.ds(k0, k1 - k0)], sem.at[g]
-        )
-
-    for g, (k0, k1) in enumerate(chunks):
-
-        def step(k, carry):
+        ks = pl.ds(g * size, size)
+        return pltpu.make_async_copy(out.at[:, ks], out_h.at[:, ks], sem.at[g])
+
+    @pl.loop(0, count)
+    def _(g):
+        def step(i, carry):
+            k = g * size + i
             for h in range(2):
                 rows = pl.ds(8 * h, 8)
                 unit = trc[0, k, rows, :] * one
@@ -706,16 +719,17 @@
                 out[1, k, rows, :] = (trc[1, k, rows, :] - cross * unit) * two
             return carry
 
-        lax.fori_loop(k0, k1, step, 0, unroll=UNROLL)
+        lax.fori_loop(0, size, step, 0, unroll=min(UNROLL, size))
         store(g).start()
+
     for h in range(2):
         rows = pl.ds(8 * h, 8)
         unit = surf[0, rows, :] * one
         sout[0, rows, :] = unit
         sout[1, rows, :] = (surf[1, rows, :] - cross * unit) * two
-    last = pltpu.make_async_copy(sout, sout_h, sem.at[len(chunks)])
+    last = pltpu.make_async_copy(sout, sout_h, sem.at[count])
     last.start()
-    for g in range(len(chunks)):
+    for g in range(count):
         store(g).wait()
     last.wait()
     grow.wait()
@@ -737,7 +751,7 @@
 
 def on_device(n, groups, tracer_pert, surface_pert, zonal_flow, merid_flow, bottom_level):
     vectors, levels, columns, rows = tracer_pert.shape
-    count = len(chunk_bounds(levels))
+    count = chunk_count(levels)
     share = shares_zonal(groups, levels)
     f32 = jnp.float32
     vmem = pl.BlockSpec(memory_space=pltpu.VMEM)

time: 36.4 us -> 36.3 us (level)
  no operation moved by 1% of the time
where the time goes in v5:
time: 36.3 us; the launch traced here: 36.1 us
  Pallas kernels  35.5 us (98%)
  between operations  0.64 us (2%)
    pallas_call x1, Pallas kernels, on_device(): pl.pallas_call(functools.partial(kernel, n, share), out_shape=(jax.ShapeD...  34.5 us
    pallas_call x1, Pallas kernels, on_device(): pl.pallas_call(scale_kernel, out_shape=(jax.ShapeDtypeStruct((vectors, le...  0.97 us

profile of v5, /device:TPU:0, one launch (start us, length us, event | category | flops | bytes accessed | tf_op | source)
XLA Modules:
  0.0 36.1 jit_solution(12462901466532272281)
XLA Ops:
  0.6 34.5 %shard_map.76 = (f32[2,50,16,128]{3,2,1,0:T(8,128)S(1)}, f32[2,16,128]{2,1,0:T(8,128)S(1)}, f32[4,8,128]{2,1,0:T(8,128)S(1)}) custom-call(f32[2,50,16,128]{3,2,1,0:T(8,128)} %bitcast.35, f32[2,16,128]{2,1,0:T(8,128)} %bitcast.38, f32[50,16,128]{2,1,0:T(8,128)} %bitcast.36, f32[50,16,128]{2,1,0:T(8,128)} %bitcast.37, s32[16,128]{1,0:T(8,128)} %bitcast.39), custom_call_target="tpu_custom_call" | custom-call | tf_op jit(solution)/shard_map/pallas_call | solution.py:761
  35.1 1.0 %shard_map.77 = (f32[2,50,16,128]{3,2,1,0:T(8,128)}, f32[2,16,128]{2,1,0:T(8,128)}, f32[3]{0:T(128)}) custom-call(f32[2,50,16,128]{3,2,1,0:T(8,128)S(1)} %get-tuple-element.9.trc, f32[2,16,128]{2,1,0:T(8,128)S(1)} %get-tuple-element.10.surf, f32[4,8,128]{2,1,0:T(8,128)S(1)} %get-tuple-element.11.tail), custom_call_target="tpu_custom_call" | custom-call | tf_op jit(solution)/shard_map/pallas_call | solution.py:813

commit v6 on v5

--- a/solution.py
+++ b/solution.py
@@ -306,8 +306,7 @@
     faces_y = [y_face(c) for c in range(2)]
     own_depth = [depths[c] for c in range(2)]
 
-    @pl.loop(0, count)
-    def _(g):
+    def first_chunk(g):
         load(1, g).wait()
         for side in range(2):
             t_copy(g, side).wait_recv()
@@ -346,8 +345,15 @@
         in_chunk(g, first, 0)
         for side in range(2):
             b_copy(g, side).start()
+
+    pl.loop(0, count - count // 3)(first_chunk)
     spread_wait(1)
     spread(2)
+    pl.loop(count - count // 3, count)(first_chunk)
+    for i in range(2, len(rounds)):
+        spread_wait(i)
+        spread(i + 1)
+    st_act(st_far, "start")
 
     face_x = {i: SURFACE_COUPLING * x_face(i) for i in range(-2, 3)}
     face_y = {i: SURFACE_COUPLING * y_face(i) for i in range(-2, 3)}
@@ -396,12 +402,7 @@
 
         return in_chunk(g, second, totals)
 
-    totals = lax.fori_loop(0, count // 2 + 1, second_chunk, (zero,) * 7)
-    for i in range(2, len(rounds)):
-        spread_wait(i)
-        spread(i + 1)
-    st_act(st_far, "start")
-    totals = lax.fori_loop(count // 2 + 1, count, second_chunk, totals)
+    totals = lax.fori_loop(0, count, second_chunk, (zero,) * 7)
 
     gain = STERIC_GAIN / levels
     for v in range(2):
@@ -489,7 +490,28 @@
 
     r_cols = [{}, {}]
 
-    @pl.when(near)
+    def forget():
+        for known in (face_x, face_y, face_s):
+            for i in [i for i in known if i not in shared_faces]:
+                del known[i]
+
+    def closing_moments():
+        tall = [{}, {}]
+        for slot in range(FAR + 3):
+            take_r(slot)
+            for c in range(2):
+                depths[c - 2 * slot] = st[slot, 2 + c]
+        take_r(SLOT[-1])
+        for slot in range(FAR + 1):
+            for v in range(2):
+                tall[v].update({-2 * slot: st[slot, 4 + v], 1 - 2 * slot: st[slot, v]})
+        cols = range(-2 * FAR, 2)
+        add_faces(cols[0] - 3, cols[-1] + 2)
+        return moments(cols, tall)
+
+    forget()
+
+    @pl.when(jnp.logical_and(near, me != 0))
     def _():
         rx_act(rx_near + rx_second, "wait_recv")
         depths[-3] = st[2, 3]
@@ -508,30 +530,17 @@
         for q in range(len(MOMENTS)):
             mo[q] = zero
 
-    for known in (face_x, face_y, face_s):
-        for i in [i for i in known if i not in shared_faces]:
-            del known[i]
+    forget()
 
     @pl.when(me == 0)
     def _():
-        rx_act(rx_far, "wait_recv")
-        tall = [{}, {}]
-        for slot in range(1, FAR + 3):
-            for c in range(2):
-                depths[c - 2 * slot] = st[slot, 2 + c]
-        for slot in range(FAR + 3):
-            take_r(slot)
-        for slot in range(1, FAR + 1):
-            for v in range(2):
-                tall[v].update({-2 * slot: st[slot, 4 + v], 1 - 2 * slot: st[slot, v]})
-        add_faces(-2 * FAR - 3, 1)
-        parts, _ = moments(range(-2 * FAR, 0), tall)
+        rx_act(rx_near + rx_second + rx_far, "wait_recv")
+        parts, powers = closing_moments()
         for q, name in enumerate(MOMENTS):
-            mo[q] = mo[q] + parts[name]
-
-    for known in (face_x, face_y, face_s):
-        for i in [i for i in known if i not in shared_faces]:
-            del known[i]
+            mo[q] = parts[name]
+        keep_powers(powers)
+
+    forget()
 
     def dot(a, b):
         return a[0] * b[0] + a[1] * b[1]
@@ -670,7 +679,7 @@
     scale_one = jnp.sqrt(gram_one + EPSILON)
     cross = gram_mix / scale_one
     rest = gram_two - 2.0 * cross * cross + cross * cross * gram_one / (gram_one + EPSILON)
-    scale_two = jnp.sqrt(rest + EPSILON)
+    scale_two = jnp.sqrt(jnp.maximum(rest, 0.0) + EPSILON)
     gout[0] = 1.0 / scale_one
     gout[1] = cross
     gout[2] = 1.0 / scale_two

time: 36.3 us -> 36.1 us (level)
  no operation moved by 1% of the time
where the time goes in v6:
time: 36.1 us; the launch traced here: 35.9 us
  Pallas kernels  35.3 us (98%)
  between operations  0.64 us (2%)
    pallas_call x1, Pallas kernels, on_device(): pl.pallas_call(functools.partial(kernel, n, share), out_shape=(jax.ShapeD...  34.3 us
    pallas_call x1, Pallas kernels, on_device(): pl.pallas_call(scale_kernel, out_shape=(jax.ShapeDtypeStruct((vectors, le...  0.97 us

profile of v6, /device:TPU:0, one launch (start us, length us, event | category | flops | bytes accessed | tf_op | source)
XLA Modules:
  0.0 35.9 jit_solution(11124536632307624250)
XLA Ops:
  0.6 34.3 %shard_map.76 = (f32[2,50,16,128]{3,2,1,0:T(8,128)S(1)}, f32[2,16,128]{2,1,0:T(8,128)S(1)}, f32[4,8,128]{2,1,0:T(8,128)S(1)}) custom-call(f32[2,50,16,128]{3,2,1,0:T(8,128)} %bitcast.35, f32[2,16,128]{2,1,0:T(8,128)} %bitcast.38, f32[50,16,128]{2,1,0:T(8,128)} %bitcast.36, f32[50,16,128]{2,1,0:T(8,128)} %bitcast.37, s32[16,128]{1,0:T(8,128)} %bitcast.39), custom_call_target="tpu_custom_call" | custom-call | tf_op jit(solution)/shard_map/pallas_call | solution.py:770
  34.9 1.0 %shard_map.77 = (f32[2,50,16,128]{3,2,1,0:T(8,128)}, f32[2,16,128]{2,1,0:T(8,128)}, f32[3]{0:T(128)}) custom-call(f32[2,50,16,128]{3,2,1,0:T(8,128)S(1)} %get-tuple-element.9.trc, f32[2,16,128]{2,1,0:T(8,128)S(1)} %get-tuple-element.10.surf, f32[4,8,128]{2,1,0:T(8,128)S(1)} %get-tuple-element.11.tail), custom_call_target="tpu_custom_call" | custom-call | tf_op jit(solution)/shard_map/pallas_call | solution.py:822

commit v7 on v6

--- a/solution.py
+++ b/solution.py
@@ -107,28 +107,26 @@
             0, size, lambda i, state: body(g * size + i, state), carry, unroll=min(UNROLL, size)
         )
 
-    def load(which, g):
-        ks = chunk(g)
-        src, dst = ((trc_h.at[:, ks], trc.at[:, ks]), (mer_h.at[ks], mer.at[ks]))[which]
-        return pltpu.make_async_copy(src, dst, in_sem.at[which, g])
+    def load(g):
+        return pltpu.make_async_copy(trc_h.at[:, chunk(g)], trc.at[:, chunk(g)], in_sem.at[5 + g])
 
     load_zon = [
-        pltpu.make_async_copy(zon_h.at[ks], zon.at[ks], in_sem.at[2, i])
+        pltpu.make_async_copy(zon_h.at[ks], zon.at[ks], in_sem.at[i])
         for i, ks in enumerate((mine, theirs))
     ]
-    load_bot = pltpu.make_async_copy(bot_h, bot, in_sem.at[3, 0])
-    load_surf = pltpu.make_async_copy(surf_h, surf, in_sem.at[3, 1])
+    load_bot = pltpu.make_async_copy(bot_h, bot, in_sem.at[2])
+    load_surf = pltpu.make_async_copy(surf_h, surf, in_sem.at[3])
+    load_mer = pltpu.make_async_copy(mer_h, mer, in_sem.at[4])
     load_zon[0].start()
     load_bot.start()
     load_surf.start()
-    load(0, 0).start()
+    load(0).start()
     load_zon[1].start()
     for g in range(1, count):
-        load(0, g).start()
-    for g in range(count):
-        load(1, g).start()
+        load(g).start()
+    load_mer.start()
     def gather_chunk(g):
-        load(0, g).wait()
+        load(g).wait()
 
         def step(k, carry):
             for c in range(2):
@@ -142,7 +140,7 @@
         return pltpu.make_async_remote_copy(
             src_ref=src.at[side, chunk(g)],
             dst_ref=dst.at[1 - side, chunk(g)],
-            send_sem=send.at[side, g],
+            send_sem=send,
             recv_sem=recv.at[1 - side, g],
             device_id={"lon": side_dev[side]},
             device_id_type=MESH,
@@ -306,8 +304,9 @@
     faces_y = [y_face(c) for c in range(2)]
     own_depth = [depths[c] for c in range(2)]
 
+    load_mer.wait()
+
     def first_chunk(g):
-        load(1, g).wait()
         for side in range(2):
             t_copy(g, side).wait_recv()
 
@@ -686,12 +685,8 @@
     gout[3] = jnp.where(lane == 0, scale_one, jnp.where(lane == 1, cross, scale_two))
 
 
-    @pl.loop(0, count)
-    def _(g):
-        for side in range(2):
-            t_copy(g, side).wait_send()
-            b_copy(g, side).wait_send()
-
+    pltpu.make_async_copy(s_t, s_t, t_send).wait()
+    pltpu.make_async_copy(s_b, s_b, b_send).wait()
     for which in range(3 if share else 2):
         z_copy(which).wait_send()
     st_act(st_near + st_far, "wait_send")
@@ -710,12 +705,12 @@
     size = levels // count
     one, cross, two = tail[0], tail[1], tail[2]
     gvec[...] = tail[3, 0, :3]
-    grow = pltpu.make_async_copy(gvec, gout_h, sem.at[count + 1])
+    grow = pltpu.make_async_copy(gvec, gout_h, sem.at[2])
     grow.start()
 
     def store(g):
         ks = pl.ds(g * size, size)
-        return pltpu.make_async_copy(out.at[:, ks], out_h.at[:, ks], sem.at[g])
+        return pltpu.make_async_copy(out.at[:, ks], out_h.at[:, ks], sem.at[0])
 
     @pl.loop(0, count)
     def _(g):
@@ -736,10 +731,9 @@
         unit = surf[0, rows, :] * one
         sout[0, rows, :] = unit
         sout[1, rows, :] = (surf[1, rows, :] - cross * unit) * two
-    last = pltpu.make_async_copy(sout, sout_h, sem.at[count])
+    last = pltpu.make_async_copy(sout, sout_h, sem.at[1])
     last.start()
-    for g in range(count):
-        store(g).wait()
+    pltpu.make_async_copy(out, out_h, sem.at[0]).wait()
     last.wait()
     grow.wait()
 
@@ -795,12 +789,12 @@
             pltpu.VMEM((16, 8, 128), f32),
             pltpu.VMEM((len(MOMENTS), 8, 128), f32),
             pltpu.VMEM((2, 3, 2, 8, 128), f32),
-            dma((4, max(2, count))),
-            dma((2, count)),
+            dma((5 + count,)),
+            dma(()),
             dma((2, count)),
             dma((zonal_sems,)),
             dma((zonal_sems,)),
-            dma((2, count)),
+            dma(()),
             dma((2, count)),
             dma((len(SLOT),)),
             dma((len(SLOT),)),
@@ -832,7 +826,7 @@
             pltpu.VMEM((vectors, levels, 16, 128), f32),
             pltpu.VMEM((vectors, 16, 128), f32),
             pltpu.VMEM((3,), f32),
-            dma((count + 2,)),
+            dma((3,)),
         ],
         compiler_params=pltpu.CompilerParams(vmem_limit_bytes=16 * 1024 * 1024),
     )(tracer, surface, tail)

time: 36.1 us -> 35.8 us (level)
  no operation moved by 1% of the time
where the time goes in v7:
time: 35.8 us; the launch traced here: 35.6 us
  Pallas kernels  35 us (98%)
  between operations  0.64 us (2%)
    pallas_call x1, Pallas kernels, on_device(): pl.pallas_call(functools.partial(kernel, n, share), out_shape=(jax.ShapeD...  34.1 us
    pallas_call x1, Pallas kernels, on_device(): pl.pallas_call(scale_kernel, out_shape=(jax.ShapeDtypeStruct((vectors, le...  0.93 us

profile of v7, /device:TPU:0, one launch (start us, length us, event | category | flops | bytes accessed | tf_op | source)
XLA Modules:
  0.0 35.6 jit_solution(4034853638797611741)
XLA Ops:
  0.6 34.1 %shard_map.76 = (f32[2,50,16,128]{3,2,1,0:T(8,128)S(1)}, f32[2,16,128]{2,1,0:T(8,128)S(1)}, f32[4,8,128]{2,1,0:T(8,128)S(1)}) custom-call(f32[2,50,16,128]{3,2,1,0:T(8,128)} %bitcast.35, f32[2,16,128]{2,1,0:T(8,128)} %bitcast.38, f32[50,16,128]{2,1,0:T(8,128)} %bitcast.36, f32[50,16,128]{2,1,0:T(8,128)} %bitcast.37, s32[16,128]{1,0:T(8,128)} %bitcast.39), custom_call_target="tpu_custom_call" | custom-call | tf_op jit(solution)/shard_map/pallas_call | solution.py:764
  34.7 0.9 %shard_map.77 = (f32[2,50,16,128]{3,2,1,0:T(8,128)}, f32[2,16,128]{2,1,0:T(8,128)}, f32[3]{0:T(128)}) custom-call(f32[2,50,16,128]{3,2,1,0:T(8,128)S(1)} %get-tuple-element.9.trc, f32[2,16,128]{2,1,0:T(8,128)S(1)} %get-tuple-element.10.surf, f32[4,8,128]{2,1,0:T(8,128)S(1)} %get-tuple-element.11.tail), custom_call_target="tpu_custom_call" | custom-call | tf_op jit(solution)/shard_map/pallas_call | solution.py:816

commit v8 on v7

--- a/solution.py
+++ b/solution.py
@@ -195,8 +195,8 @@
         return pltpu.make_async_remote_copy(
             src_ref=buf.at[0, part],
             dst_ref=buf.at[SLOT[s], part],
-            send_sem=send.at[SLOT[s]],
-            recv_sem=recv.at[SLOT[s]],
+            send_sem=send.at[s % 4 if s < 3 else 0],
+            recv_sem=recv.at[SLOT[s] - 1],
             device_id=lon_peer(s),
             device_id_type=MESH,
         )
@@ -796,10 +796,10 @@
             dma((zonal_sems,)),
             dma(()),
             dma((2, count)),
-            dma((len(SLOT),)),
-            dma((len(SLOT),)),
-            dma((len(SLOT),)),
-            dma((len(SLOT),)),
+            dma((4,)),
+            dma((len(SLOT) - 1,)),
+            dma((4,)),
+            dma((len(SLOT) - 1,)),
             dma(()),
             dma(()),
             pltpu.SemaphoreType.REGULAR((max(1, len(spread_rounds(n))),)),

time: 35.8 us -> 35.7 us (level)
  no operation moved by 1% of the time
where the time goes in v8:
time: 35.7 us; the launch traced here: 35.5 us
  Pallas kernels  34.9 us (98%)
  between operations  0.64 us (2%)
    pallas_call x1, Pallas kernels, on_device(): pl.pallas_call(functools.partial(kernel, n, share), out_shape=(jax.ShapeD...  34 us
    pallas_call x1, Pallas kernels, on_device(): pl.pallas_call(scale_kernel, out_shape=(jax.ShapeDtypeStruct((vectors, le...  0.93 us

profile of v8, /device:TPU:0, one launch (start us, length us, event | category | flops | bytes accessed | tf_op | source)
XLA Modules:
  0.0 35.5 jit_solution(10214501989618899765)
XLA Ops:
  0.6 34.0 %shard_map.76 = (f32[2,50,16,128]{3,2,1,0:T(8,128)S(1)}, f32[2,16,128]{2,1,0:T(8,128)S(1)}, f32[4,8,128]{2,1,0:T(8,128)S(1)}) custom-call(f32[2,50,16,128]{3,2,1,0:T(8,128)} %bitcast.35, f32[2,16,128]{2,1,0:T(8,128)} %bitcast.38, f32[50,16,128]{2,1,0:T(8,128)} %bitcast.36, f32[50,16,128]{2,1,0:T(8,128)} %bitcast.37, s32[16,128]{1,0:T(8,128)} %bitcast.39), custom_call_target="tpu_custom_call" | custom-call | tf_op jit(solution)/shard_map/pallas_call | solution.py:764
  34.6 0.9 %shard_map.77 = (f32[2,50,16,128]{3,2,1,0:T(8,128)}, f32[2,16,128]{2,1,0:T(8,128)}, f32[3]{0:T(128)}) custom-call(f32[2,50,16,128]{3,2,1,0:T(8,128)S(1)} %get-tuple-element.9.trc, f32[2,16,128]{2,1,0:T(8,128)S(1)} %get-tuple-element.10.surf, f32[4,8,128]{2,1,0:T(8,128)S(1)} %get-tuple-element.11.tail), custom_call_target="tpu_custom_call" | custom-call | tf_op jit(solution)/shard_map/pallas_call | solution.py:816
